TPU v7x, 512 devices: a whole 4x8x8 slice. The times are simulated.
512 devices in a mesh: seq: 128 (over y, z, core), tp: 4 (over x).
Axes of the slice: x: 4, y: 8, z: 8, core: 2. Of those that a mesh axis runs over, the one named last changes fastest.
Arguments:
- hidden_in: bfloat16 [16, 1024], P(None, 'tp'), may hold values from -6 to 6
- w_qkv: bfloat16 [3, 1024, 1024], P(None, None, 'tp'), may hold values from -0.1875 to 0.1875
- w_out: bfloat16 [1024, 1024], P('tp'), may hold values from -0.1875 to 0.1875
- key_cache: bfloat16 [16, 8192, 1024], P(None, 'seq', 'tp'), may hold values from -400 to 400
- value_cache: bfloat16 [16, 8192, 1024], P(None, 'seq', 'tp'), may hold values from -24 to 24
- lengths: int32 [16], replicated, may hold values from 256 to 8191, as said below
- ln_gain: float32 [1024], P('tp'), may hold values from 0.1 to 1.9
- ln_bias: float32 [1024], P('tp'), may hold values from -3 to 3
Outputs:
- layer_out: bfloat16 [16, 1024], P(None, 'tp')
- keys_out: bfloat16 [16, 8192, 1024], P(None, 'seq', 'tp')
- values_out: bfloat16 [16, 8192, 1024], P(None, 'seq', 'tp')
Inputs may be any that keep to these rules, and one draw needn't show every extreme that they name: `lengths`: the shortest and the longest of these both occur in every draw.
All inputs are finite; a program needn't handle non-finite values.
Results may differ from a plain program's by a relative error of at most 0.0094.
Values may be sent and summed in bfloat16 or wider, within the bound.
A program may use at most 64 MiB of HBM per device.

v0:
```python
import jax
import jax.numpy as jnp
from jax import lax
from jax.sharding import PartitionSpec as P

D = 1024
HD = 64


def body(hidden_in, w_qkv, w_out, key_cache, value_cache, lengths, ln_gain, ln_bias):
    batch_rows, local_width = hidden_in.shape
    span_local = key_cache.shape[1]
    heads_local = local_width // HD
    features = lax.all_gather(hidden_in, "tp", axis=1, tiled=True)
    projected = jnp.einsum(
        "bd,kdc->kbc", features, w_qkv, preferred_element_type=jnp.float32
    ).astype(jnp.bfloat16)
    query, new_key, new_value = (projected[0], projected[1], projected[2])
    first_pos = lax.axis_index("seq") * span_local
    positions = first_pos + jnp.arange(span_local, dtype=jnp.int32)
    hit = positions[None, :] == lengths[:, None]
    keys_out = jnp.where(hit[:, :, None], new_key[:, None, :], key_cache)
    values_out = jnp.where(hit[:, :, None], new_value[:, None, :], value_cache)
    valid = (positions[None, :] <= lengths[:, None])[:, None, :]
    query_heads = query.reshape(batch_rows, heads_local, HD)
    key_heads = keys_out.reshape(batch_rows, span_local, heads_local, HD)
    value_heads = values_out.reshape(batch_rows, span_local, heads_local, HD)
    scores = jnp.einsum(
        "bhd,bphd->bhp", query_heads, key_heads, preferred_element_type=jnp.float32
    ) * HD ** (-0.5)
    local_top = jnp.max(jnp.where(valid, scores, -1e30), axis=2)
    top_all = lax.pmax(local_top, "seq")
    weights = jnp.where(valid, jnp.exp(scores - top_all[:, :, None]), jnp.float32(0.0))
    total_part = jnp.sum(weights, axis=2)
    summed_part = jnp.einsum(
        "bhp,bphd->bhd",
        weights,
        value_heads,
        preferred_element_type=jnp.float32,
        precision=lax.Precision.HIGHEST,
    )
    total_part, summed_part = (total_part, summed_part.reshape(batch_rows, local_width))
    total_all, summed_all = lax.psum((total_part, summed_part), "seq")
    attended = (summed_all / jnp.repeat(total_all, HD, axis=1)).astype(jnp.bfloat16)
    mixed_cols = lax.psum_scatter(
        lax.dot_general(
            w_out, attended, (((0,), (1,)), ((), ())), preferred_element_type=jnp.float32
        ),
        "tp",
        scatter_dimension=0,
        tiled=True,
    )
    resid = hidden_in.astype(jnp.float32) + mixed_cols.T
    total_sum = lax.psum(jnp.sum(resid, axis=1), "tp")
    mean_val = (total_sum / D)[:, None]
    centred = resid - mean_val
    var_val = (lax.psum(jnp.sum(centred * centred, axis=1), "tp") / D)[:, None]
    normed = centred / jnp.sqrt(var_val + 1e-05) * ln_gain + ln_bias
    return (normed.astype(jnp.bfloat16), keys_out, values_out)


def solution(mesh):
    in_specs = (
        P(None, "tp"),
        P(None, None, "tp"),
        P("tp", None),
        P(None, "seq", "tp"),
        P(None, "seq", "tp"),
        P(),
        P("tp"),
        P("tp"),
    )
    out_specs = (P(None, "tp"), P(None, "seq", "tp"), P(None, "seq", "tp"))
    return jax.shard_map(body, mesh=mesh, in_specs=in_specs, out_specs=out_specs, check_vma=False)
```

profile of v0, /device:TPU:1, one launch (start us, length us, event | category | flops | bytes accessed | tf_op | source)
XLA Modules:
  0.0 816.2 jit_solution(3064783224928968697)
XLA Ops:
  7.2 0.0 copy-start
  7.2 0.0 copy-start.8
  7.2 0.0 copy-start.3
  7.2 0.0 reduce-scatter.2.cloned.1.call-start
  7.3 10.5 %all_gather.3 = bf16[16,1024]{1,0:T(8,128)(2,1)S(1)} all-gather(bf16[16,256]{1,0:T(8,128)(2,1)} %param.8), channel_id=1, replica_groups=mesh['seq'=128,'tp'=4] {'tp'}, dimensions={1}, use_global_device_ids=true | all-gather | bytes 40960 | tf_op jit(solution)/shard_map/all_gather | solution.py:14
  17.8 0.0 copy-done
  17.8 0.3 fusion
  18.1 0.1 reshape.90
  18.2 0.0 copy-done.8
  18.2 0.1 broadcast_compare_fusion.1
  18.3 0.0 copy-done.3
  18.3 1.2 broadcast_select_fusion.1
  19.6 0.0 copy-start.1
  19.6 0.0 copy-start.2
  19.6 1.3 copy.18
  20.9 1.6 fusion.8
  22.5 0.0 copy-start.4
  22.5 0.1 select_reduce_fusion
  22.6 256.7 %pmax.7 = f32[16,4]{0,1:T(4,128)S(1)} all-reduce(f32[16,4]{0,1:T(4,128)S(1)} %select_reduce_fusion), channel_id=1, replica_groups=mesh['seq'=128,'tp'=4] {'seq'}, use_global_device_ids=true, to_apply=%region_1.2 | all-reduce | flops 64 | bytes 512 | tf_op jit(solution)/shard_map/pmax | solution.py:32
  279.3 0.2 fusion.5
  279.5 0.0 copy-start.5
  279.5 0.0 copy-start.6
  279.5 0.0 copy-start.7
  279.5 1.4 reshape.81
  280.9 0.0 copy-done.1
  280.9 0.0 copy-done.2
  280.9 2.1 fusion.1
  283.1 0.1 reshape.82
  283.2 487.4 %all-reduce = (f32[16,256]{1,0:T(8,128)S(1)}, f32[16,4]{0,1:T(4,128)S(1)}) all-reduce(f32[16,256]{1,0:T(8,128)S(1)} %reshape.82, f32[16,4]{0,1:T(4,128)S(1)} %get-tuple-element.5), channel_id=1, replica_groups=mesh['seq'=128,'tp'=4] {'seq'}, use_global_device_ids=true, to_apply=%region_2.3 | all-reduce | flops 4160 | bytes 33280 | tf_op jit(solution)/shard_map/psum | solution.py:43
  770.5 0.1 copy.11
  770.6 0.1 broadcast_in_dim.73
  770.7 0.1 reshape.83
  770.8 0.0 copy-done.4
  770.8 0.8 convolution_bitcast_fusion
  771.6 0.0 reduce-scatter.2.cloned.1.call-update
  771.6 21.1 %reduce-scatter.2.cloned.1.call-done = f32[256,16]{0,1:T(8,128)} async-done(((f32[1024,16]{0,1:T(8,128)}), f32[256,16]{0,1:T(8,128)}) %reduce-scatter.2.cloned.1.call-update) | async-done | bytes 16400 | tf_op jit(solution)/shard_map/reduce_scatter | solution.py:45
  792.8 0.0 copy-done.5
  792.8 0.8 fusion.7
  793.6 6.8 psum.30
  800.4 0.9 multiply_reduce_fusion
  801.3 6.6 psum.31
  808.0 0.0 copy-done.6
  808.0 0.0 copy-done.7
  808.0 1.4 add_convert_fusion
  (4 shorter events, 0.0 us)
Async XLA Ops:
  7.2 10.6 %copy-start = (bf16[3,1024,256]{2,1,0:T(8,128)(2,1)S(1)}, bf16[3,1024,256]{2,1,0:T(8,128)(2,1)}, u32[]{:S(2)}) copy-start(bf16[3,1024,256]{2,1,0:T(8,128)(2,1)} %param.9) | copy-start | bytes 4718596
  7.2 11.0 %copy-start.8 = (s32[16]{0:T(128)S(1)}, s32[16]{0:T(128)}, u32[]{:S(2)}) copy-start(s32[16]{0:T(128)} %param.13) | copy-start | bytes 196
  7.2 11.1 %copy-start.3 = (bf16[16,64,256]{2,1,0:T(8,128)(2,1)S(1)}, bf16[16,64,256]{2,1,0:T(8,128)(2,1)}, u32[]{:S(2)}) copy-start(bf16[16,64,256]{2,1,0:T(8,128)(2,1)} %param.11) | copy-start | bytes 1572868
  7.2 785.6 %reduce-scatter.2.cloned.1.call-start = ((), (), s32[]{:S(2)}) async-start(), calls=%async_computation.1 | async-start | bytes 81920 | tf_op jit(solution)/shard_map/reduce_scatter | solution.py:45
  19.6 261.4 %copy-start.1 = (bf16[16,64,256]{2,1,0:T(8,128)(2,1)}, bf16[16,64,256]{2,1,0:T(8,128)(2,1)S(1)}, u32[]{:S(2)}) copy-start(bf16[16,64,256]{2,1,0:T(8,128)(2,1)S(1)} %get-tuple-element.10) | copy-start | bytes 1572868
  19.6 261.4 %copy-start.2 = (bf16[16,64,256]{2,1,0:T(8,128)(2,1)}, bf16[16,64,256]{2,1,0:T(8,128)(2,1)S(1)}, u32[]{:S(2)}) copy-start(bf16[16,64,256]{2,1,0:T(8,128)(2,1)S(1)} %get-tuple-element.11) | copy-start | bytes 1572868
  22.5 748.3 %copy-start.4 = (bf16[256,1024]{1,0:T(8,128)(2,1)S(1)}, bf16[256,1024]{1,0:T(8,128)(2,1)}, u32[]{:S(2)}) copy-start(bf16[256,1024]{1,0:T(8,128)(2,1)} %param.10) | copy-start | bytes 1572868
  279.5 513.3 %copy-start.5 = (bf16[16,256]{1,0:T(8,128)(2,1)S(1)}, bf16[16,256]{1,0:T(8,128)(2,1)}, u32[]{:S(2)}) copy-start(bf16[16,256]{1,0:T(8,128)(2,1)} %param.8) | copy-start | bytes 24580
  279.5 528.4 %copy-start.6 = (f32[256]{0:T(256)S(1)}, f32[256]{0:T(256)}, u32[]{:S(2)}) copy-start(f32[256]{0:T(256)} %param.15) | copy-start | bytes 3076
  279.5 528.4 %copy-start.7 = (f32[256]{0:T(256)S(1)}, f32[256]{0:T(256)}, u32[]{:S(2)}) copy-start(f32[256]{0:T(256)} %param.14) | copy-start | bytes 3076
Sparse Core Ops, SparseCore 0:
  771.7 20.9 reduce-scatter.1
where the time goes:
time: 822 us; the launch traced here: 816 us
  blocking collectives  768 us (93%)
  waiting for transfers between devices  21.1 us (3%)
  between operations  14.1 us (2%)
    psum x1, blocking collectives, body(): total_all, summed_all = lax.psum((total_part, summed_part), 'seq')  487 us
    pmax x1, blocking collectives, body(): top_all = lax.pmax(local_top, 'seq')  257 us
    reduce_scatter x1, waiting for transfers between devices, body(): lax.psum_scatter(lax.dot_general(w_out, attended, (((0,), (1,)), ((), ())...  21.1 us
  transfers between devices with their start and end apart: 1, of which 1 were waited for; matrix products, arithmetic and copies ran while one was open for 0% of the time, Pallas kernels for 0%

commit v1 on v0

v1 whole, which is shorter than its diff:
```python
import jax
import jax.numpy as jnp
from jax import lax
from jax.experimental import pallas as pl
from jax.experimental.pallas import tpu as pltpu
from jax.sharding import PartitionSpec as P

D = 1024
HD = 64
B = 16
W = 256
TP = 4
SPAN = 64
NEG = -1e30
F32 = jnp.float32
BF16 = jnp.bfloat16
MESH = pl.DeviceIdType.MESH


def tile_at(ref, index):
    return ref.at[pl.ds(pl.multiple_of(index * 8, 8), 8), :]


def merge(tiles):
    top = tiles[0]
    for tile in tiles[1:]:
        top = jnp.maximum(top, tile)
    total = None
    for tile in tiles:
        factor = pltpu.roll(jnp.exp(tile - top), 4, 0)
        total = tile * factor if total is None else total + tile * factor
    row = lax.broadcasted_iota(jnp.int32, (8, 128), 0)
    return jnp.where(row < 4, total, top)


def kernel(
    lens, hid, wqkv, wout, kc, vc, gain, bias,
    out, kout, vout,
    gath, wbuf, wobuf, kbuf, vbuf, gbuf, bbuf,
    send, rs, zb, newb, hidb, mixb, ag,
    lsem, h_s, h_r, rs_s, rs_r, z_s, z_r, m_s, m_r, a_s, a_r,
):
    seq = lax.axis_index("seq")
    tp = lax.axis_index("tp")
    y, z, c = seq // 16, (seq % 16) // 2, seq % 2
    mine = y * 2 + c

    loads = [
        pltpu.make_async_copy(hid, gath.at[tp], lsem.at[0]),
        pltpu.make_async_copy(wqkv.at[0], wbuf.at[0], lsem.at[1]),
        pltpu.make_async_copy(kc, kbuf, lsem.at[2]),
        pltpu.make_async_copy(vc, vbuf, lsem.at[3]),
        pltpu.make_async_copy(wqkv.at[1], wbuf.at[1], lsem.at[4]),
        pltpu.make_async_copy(wqkv.at[2], wbuf.at[2], lsem.at[5]),
        pltpu.make_async_copy(wout, wobuf, lsem.at[6]),
        pltpu.make_async_copy(gain, gbuf, lsem.at[7]),
        pltpu.make_async_copy(bias, bbuf, lsem.at[8]),
    ]
    for load in loads:
        load.start()

    tp_peers = [lax.rem(tp + d, TP) for d in range(1, TP)]
    yc_peers = []
    for k in range(1, 16):
        y2 = lax.rem(y + k // 2, 8)
        c2 = lax.rem(c + k % 2, 2)
        yc_peers.append((k, y2 * 16 + z * 2 + c2, y2 * 2 + c2))
    z_peers = []
    for d in range(1, 8):
        z2 = lax.rem(z + d, 8)
        z_peers.append((z2, y * 16 + z2 * 2 + c))

    barrier = pltpu.get_barrier_semaphore()
    for t in tp_peers:
        pl.semaphore_signal(barrier, inc=1, device_id=(seq, t), device_id_type=MESH)
    for _, s, _ in yc_peers:
        pl.semaphore_signal(barrier, inc=1, device_id=(s, tp), device_id_type=MESH)
    for _, s in z_peers:
        pl.semaphore_signal(barrier, inc=1, device_id=(s, tp), device_id_type=MESH)
    loads[0].wait()
    pl.semaphore_wait(barrier, 25)

    sends = []
    for d, t in enumerate(tp_peers):
        copy = pltpu.make_async_remote_copy(
            gath.at[tp], gath.at[tp], h_s.at[d], h_r.at[tp], device_id=(seq, t), device_id_type=MESH
        )
        copy.start()
        sends.append(copy)
    loads[1].wait()

    def project(index, t):
        rows = pl.ds(pl.multiple_of(t * W, W), W)
        return jnp.dot(gath[t], wbuf[index, rows, :], preferred_element_type=F32)

    acc = project(0, tp)
    for t in tp_peers:
        pltpu.make_async_remote_copy(
            gath.at[t], gath.at[t], h_s.at[0], h_r.at[t], device_id=(seq, t), device_id_type=MESH
        ).wait_recv()
        acc = acc + project(0, t)
    query = acc.astype(BF16)

    column_head = lax.broadcasted_iota(jnp.int32, (B, W), 1) // HD
    spread = jnp.concatenate(
        [jnp.where(column_head == h, query.astype(F32), 0.0) for h in range(TP)], axis=0
    ).astype(BF16)
    row_b = lax.broadcasted_iota(jnp.int32, (B, 1), 0)
    local_len = jnp.zeros((B, 1), jnp.int32)
    for b in range(B):
        local_len = jnp.where(row_b == b, lens[b] - seq * SPAN, local_len)
    low = jnp.concatenate([row_b * SPAN] * 4, axis=0)
    high = low + jnp.concatenate([jnp.clip(local_len, 0, SPAN)] * 4, axis=0)
    column = lax.broadcasted_iota(jnp.int32, (4 * B, B * SPAN), 1)
    valid = jnp.logical_and(column >= low, column < high)
    loads[2].wait()
    keys = kbuf[...].reshape(B * SPAN, W)
    scores = lax.dot_general(spread, keys, (((1,), (1,)), ((), ())), preferred_element_type=F32)
    scores = jnp.where(valid, scores * HD ** (-0.5), NEG)
    top = jnp.max(scores, axis=1, keepdims=True)
    weights = jnp.where(valid, jnp.exp(scores - top), 0.0)
    total = jnp.sum(weights, axis=1, keepdims=True)
    upper = weights.astype(BF16)
    lower = (weights - upper.astype(F32)).astype(BF16)
    loads[3].wait()
    values = vbuf[...].reshape(B * SPAN, W)
    both = jnp.dot(jnp.concatenate([upper, lower], axis=0), values, preferred_element_type=F32)
    summed = both[: 4 * B] + both[4 * B :]

    def fold(rows):
        result = jnp.broadcast_to(rows[0:B], (B, W))
        for h in range(1, 4):
            result = jnp.where(column_head == h, rows[h * B : (h + 1) * B], result)
        return result

    def store_tiles(ref, values16, totals16, tops16):
        for part in range(2):
            lanes = slice(part * 128, part * 128 + 128)
            ref[pl.ds(part, B, stride=8), :] = values16[:, lanes]
            ref[pl.ds(2 + part, B, stride=8), :] = totals16[:, lanes]
            ref[pl.ds(4 + part, B, stride=8), :] = tops16[:, lanes]
            ref[pl.ds(6 + part, B, stride=8), :] = tops16[:, lanes]

    store_tiles(send, fold(summed), fold(total), fold(top))
    for k, s, request in yc_peers:
        copy = pltpu.make_async_remote_copy(
            tile_at(send, request), tile_at(rs, k), rs_s.at[k], rs_r.at[k],
            device_id=(s, tp), device_id_type=MESH,
        )
        copy.start()
        sends.append(copy)

    loads[4].wait()
    loads[5].wait()
    new_key = sum(project(1, t) for t in range(TP)).astype(BF16)
    new_value = sum(project(2, t) for t in range(TP)).astype(BF16)
    product = query.astype(F32) * new_key.astype(F32)
    product_up = product.astype(BF16)
    product_low = (product - product_up.astype(F32)).astype(BF16)
    same_head = (
        lax.broadcasted_iota(jnp.int32, (W, W), 0) // HD == lax.broadcasted_iota(jnp.int32, (W, W), 1) // HD
    )
    ones = jnp.where(same_head, 1.0, 0.0).astype(BF16)
    new_both = jnp.dot(jnp.concatenate([product_up, product_low], axis=0), ones, preferred_element_type=F32)
    new_score = (new_both[:B] + new_both[B:]) * HD ** (-0.5)
    store_tiles(newb, new_value.astype(F32), jnp.ones((B, W), F32), new_score)

    position = lax.broadcasted_iota(jnp.int32, (SPAN, W), 0)
    for b in range(B):
        hit = position == lens[b] - seq * SPAN
        kout[b] = jnp.where(hit, new_key[b : b + 1].astype(F32), kbuf[b].astype(F32)).astype(BF16)
        vout[b] = jnp.where(hit, new_value[b : b + 1].astype(F32), vbuf[b].astype(F32)).astype(BF16)
    for t in range(TP):
        state = gath[t].astype(F32)
        for part in range(2):
            hidb[pl.ds(t * 2 + part, B, stride=8), :] = state[:, part * 128 : part * 128 + 128]

    tiles = [tile_at(send, mine)[...]]
    for k, s, request in yc_peers:
        pltpu.make_async_remote_copy(
            tile_at(send, request), tile_at(rs, k), rs_s.at[k], rs_r.at[k],
            device_id=(s, tp), device_id_type=MESH,
        ).wait_recv()
        tiles.append(rs[k * 8 : k * 8 + 8, :])
    tile_at(zb, z)[...] = merge(tiles)

    for d, (_, s) in enumerate(z_peers):
        copy = pltpu.make_async_remote_copy(
            tile_at(zb, z), tile_at(zb, z), z_s.at[d], z_r.at[z], device_id=(s, tp), device_id_type=MESH
        )
        copy.start()
        sends.append(copy)
    loads[6].wait()
    for z2, s in z_peers:
        pltpu.make_async_remote_copy(
            tile_at(zb, z2), tile_at(zb, z2), z_s.at[0], z_r.at[z2], device_id=(s, tp), device_id_type=MESH
        ).wait_recv()
    merged = merge([zb[k * 8 : k * 8 + 8, :] for k in range(8)] + [tile_at(newb, mine)[...]])

    attended = merged / pltpu.roll(merged, 6, 0)
    first = attended[0:1]
    second = attended[1:2]
    row_vec = jnp.concatenate([first, second], axis=1).astype(BF16)
    mixed = jnp.dot(
        jnp.broadcast_to(row_vec, (16, W)), wobuf[...], preferred_element_type=F32
    )
    base = pl.multiple_of(tp * 8, 8)
    mixb[pl.ds(base, 8), :] = jnp.concatenate(
        [mixed[0:1, j * 128 : j * 128 + 128] for j in range(8)], axis=0
    )
    for d, t in enumerate(tp_peers):
        copy = pltpu.make_async_remote_copy(
            tile_at(mixb, tp), tile_at(mixb, tp), m_s.at[d], m_r.at[tp], device_id=(seq, t), device_id_type=MESH
        )
        copy.start()
        sends.append(copy)
    loads[7].wait()
    loads[8].wait()
    for t in tp_peers:
        pltpu.make_async_remote_copy(
            tile_at(mixb, t), tile_at(mixb, t), m_s.at[0], m_r.at[t], device_id=(seq, t), device_id_type=MESH
        ).wait_recv()
    resid = tile_at(hidb, mine)[...] + (
        (mixb[0:8, :] + mixb[8:16, :]) + (mixb[16:24, :] + mixb[24:32, :])
    )
    mean = jnp.sum(jnp.sum(resid, axis=0, keepdims=True), axis=1, keepdims=True) / D
    centred = resid - mean
    var = jnp.sum(jnp.sum(centred * centred, axis=0, keepdims=True), axis=1, keepdims=True) / D
    scaled = centred / jnp.sqrt(var + 1e-05)
    own = scaled[0:2]
    for t in range(1, TP):
        own = jnp.where(tp == t, scaled[2 * t : 2 * t + 2], own)
    normed = own * gbuf[...] + bbuf[...]
    ag[pl.ds(pl.multiple_of(mine * 8, 8), 2), :] = normed
    for k, s, request in yc_peers:
        copy = pltpu.make_async_remote_copy(
            tile_at(ag, mine), tile_at(ag, mine), a_s.at[k], a_r.at[mine],
            device_id=(s, tp), device_id_type=MESH,
        )
        copy.start()
        sends.append(copy)
    for k, s, request in yc_peers:
        pltpu.make_async_remote_copy(
            tile_at(ag, request), tile_at(ag, request), a_s.at[k], a_r.at[request],
            device_id=(s, tp), device_id_type=MESH,
        ).wait_recv()
    for part in range(2):
        out[:, part * 128 : part * 128 + 128] = ag[pl.ds(part, B, stride=8), :].astype(BF16)
    for copy in sends:
        copy.wait_send()


def body(hidden_in, w_qkv, w_out, key_cache, value_cache, lengths, ln_gain, ln_bias):
    hbm = pl.BlockSpec(memory_space=pl.ANY)
    vmem = pl.BlockSpec(memory_space=pltpu.VMEM)
    cache = jax.ShapeDtypeStruct((B, SPAN, W), BF16)
    dma = pltpu.SemaphoreType.DMA
    return pl.pallas_call(
        kernel,
        out_shape=(jax.ShapeDtypeStruct((B, W), BF16), cache, cache),
        in_specs=[pl.BlockSpec(memory_space=pltpu.SMEM)] + [hbm] * 7,
        out_specs=(vmem, vmem, vmem),
        scratch_shapes=[
            pltpu.VMEM((TP, B, W), BF16),
            pltpu.VMEM((3, D, W), BF16),
            pltpu.VMEM((W, D), BF16),
            pltpu.VMEM((B, SPAN, W), BF16),
            pltpu.VMEM((B, SPAN, W), BF16),
            pltpu.VMEM((2, 128), F32),
            pltpu.VMEM((2, 128), F32),
            pltpu.VMEM((128, 128), F32),
            pltpu.VMEM((128, 128), F32),
            pltpu.VMEM((64, 128), F32),
            pltpu.VMEM((128, 128), F32),
            pltpu.VMEM((128, 128), F32),
            pltpu.VMEM((32, 128), F32),
            pltpu.VMEM((128, 128), F32),
            dma((9,)),
            dma((3,)), dma((4,)),
            dma((16,)), dma((16,)),
            dma((7,)), dma((8,)),
            dma((3,)), dma((4,)),
            dma((16,)), dma((16,)),
        ],
        compiler_params=pltpu.CompilerParams(collective_id=0, has_side_effects=True),
        name="sublayer",
    )(
        lengths, hidden_in, w_qkv, w_out, key_cache, value_cache,
        ln_gain.reshape(2, 128), ln_bias.reshape(2, 128),
    )


def solution(mesh):
    in_specs = (
        P(None, "tp"),
        P(None, None, "tp"),
        P("tp", None),
        P(None, "seq", "tp"),
        P(None, "seq", "tp"),
        P(),
        P("tp"),
        P("tp"),
    )
    out_specs = (P(None, "tp"), P(None, "seq", "tp"), P(None, "seq", "tp"))
    return jax.shard_map(body, mesh=mesh, in_specs=in_specs, out_specs=out_specs, check_vma=False)
```

time: 822 us -> 46.3 us (0.06)
  blocking collectives: 768 us -> 0 us
  Pallas kernels: 0 us -> 40.3 us
  waiting for transfers between devices: 21.1 us -> 0 us
  between operations: 14.1 us -> 0.64 us
    psum x3 -> x0, blocking collectives: 501 us -> none  [the longest x1 487 us: body(): total_all, summed_all = lax.psum((total_part, summed_part), 'seq')]
    pmax x1 -> x0, blocking collectives: 257 us -> none  [body(): top_all = lax.pmax(local_top, 'seq')]
    pallas_call x0 -> x1, Pallas kernels: none -> 40.3 us  [body(): pl.pallas_call(kernel, out_shape=(jax.ShapeDtypeStruct((B, W), BF16), cac...]
    reduce_scatter x1 -> x0, waiting for transfers between devices: 21.1 us -> none  [body(): lax.psum_scatter(lax.dot_general(w_out, attended, (((0,), (1,)), ((), ())...]
    all_gather x1 -> x0, blocking collectives: 10.5 us -> none  [body(): features = lax.all_gather(hidden_in, 'tp', axis=1, tiled=True)]
  transfers between devices with their start and end apart: 1 -> 0, of which waited for: 1 -> 0; matrix products, arithmetic and copies ran while one was open for 0% -> 0% of each run, Pallas kernels for 0% -> 0%
where the time goes in v1:
time: 46.3 us; the launch traced here: 46 us
  Pallas kernels  40.3 us (87%)
  local copies, waits for them, and re-layouts  5.06 us (11%)
  between operations  0.64 us (1%)
    pallas_call x1, Pallas kernels, body(): pl.pallas_call(kernel, out_shape=(jax.ShapeDtypeStruct((B, W), BF16), cac...  40.3 us
    unnamed x3, local copies, waits for them, and re-layouts  5.06 us

profile of v1, /device:TPU:1, one launch (start us, length us, event | category | flops | bytes accessed | tf_op | source)
XLA Modules:
  0.0 46.0 jit_solution(9228820621058859474)
XLA Ops:
  0.6 40.3 %sublayer.1 = (bf16[16,256]{1,0:T(8,128)(2,1)}, bf16[16,64,256]{2,1,0:T(8,128)(2,1)}, bf16[16,64,256]{2,1,0:T(8,128)(2,1)}) custom-call(s32[16]{0:T(128)} %lens.1, bf16[16,256]{1,0:T(8,128)(2,1)} %hid.1, bf16[3,1024,256]{2,1,0:T(8,128)(2,1)} %wqkv.1, bf16[256,1024]{1,0:T(8,128)(2,1)} %wout.1, bf16[16,64,256]{2,1,0:T(8,128)(2,1)} %kc.1, ...), custom_call_target="tpu_custom_call" | custom-call | tf_op jit(solution)/shard_map/sublayer/pallas_call | solution.py:258
  41.0 1.3 %copy.14 = bf16[16,256]{1,0:T(8,128)(2,1)} copy(bf16[16,256]{1,0:T(8,128)(2,1)} %get-tuple-element.6) | data formatting | bytes 16384
  42.2 1.9 %copy.15 = bf16[16,64,256]{2,1,0:T(8,128)(2,1)} copy(bf16[16,64,256]{2,1,0:T(8,128)(2,1)} %get-tuple-element.7) | data formatting | bytes 1048576
  44.1 1.9 %copy.16 = bf16[16,64,256]{2,1,0:T(8,128)(2,1)} copy(bf16[16,64,256]{2,1,0:T(8,128)(2,1)} %get-tuple-element.8) | data formatting | bytes 1048576

commit v2 on v0

v2 whole, which is shorter than its diff:
```python
import jax
import jax.numpy as jnp
from jax import lax
from jax.experimental import pallas as pl
from jax.experimental.pallas import tpu as pltpu
from jax.sharding import PartitionSpec as P

D = 1024
HD = 64
B = 16
HALF = 8
W = 256
TP = 4
RING = 8
SPAN = 64
SLOT = 24
SENT = 17
NEG = -1e30
F32 = jnp.float32
BF16 = jnp.bfloat16
MESH = pl.DeviceIdType.MESH


def iota(shape, dim):
    return lax.broadcasted_iota(jnp.int32, shape, dim)


def split_dot(rows, matrix):
    upper = rows.astype(BF16)
    lower = (rows - upper.astype(F32)).astype(BF16)
    both = jnp.dot(jnp.concatenate([upper, lower], axis=0), matrix, preferred_element_type=F32)
    return both[: rows.shape[0]] + both[rows.shape[0] :]


def to_row(tops, totals):
    lane, request = iota((HALF, W), 1) % HD, iota((HALF, W), 0)
    picked = jnp.where(lane == request, tops, jnp.where(lane == request + HALF, totals, 0.0))
    row = jnp.sum(picked, axis=0, keepdims=True)
    return row[:, :128] + pltpu.roll(row[:, 128:], 16, 1)


def spread_rows(rows):
    entry = iota((HALF, 128), 1)
    keep = jnp.logical_and(entry % 16 == iota((HALF, 128), 0), entry % 64 < 32)
    picked = jnp.concatenate(
        [jnp.where(keep, rows[s : s + 1], 0.0) for s in range(rows.shape[0])], axis=0
    )
    lane, column = iota((128, W), 0), iota((128, W), 1)
    head = lane // 64 + 2 * ((lane % 64) // 16)
    matrix = jnp.where(jnp.logical_and(lane % 64 < 32, head == column // HD), 1.0, 0.0).astype(BF16)
    return split_dot(picked, matrix)


def kernel(
    lens, hid, wqkv, wout, kc, vc, gain, bias,
    out, kout, vout,
    gath, wbuf, wobuf, kbuf, vbuf, gbuf, bbuf,
    csend, crecv, yb, zb, mixb, fin, obuf,
    lsem, hsem, recv, sent,
):
    seq = lax.axis_index("seq")
    tp = lax.axis_index("tp")
    y, z, c = seq // 16, (seq % 16) // 2, seq % 2

    loads = [
        pltpu.make_async_copy(hid, gath.at[tp], lsem.at[0]),
        pltpu.make_async_copy(wqkv.at[0], wbuf.at[0], lsem.at[1]),
        pltpu.make_async_copy(kc, kbuf, lsem.at[2]),
        pltpu.make_async_copy(vc, vbuf, lsem.at[3]),
        pltpu.make_async_copy(wqkv.at[pl.ds(1, 2)], wbuf.at[pl.ds(1, 2)], lsem.at[4]),
        pltpu.make_async_copy(wout, wobuf, lsem.at[5]),
        pltpu.make_async_copy(gain, gbuf, lsem.at[6]),
        pltpu.make_async_copy(bias, bbuf, lsem.at[7]),
    ]
    for load in loads:
        load.start()

    tp_peers = [(seq, lax.rem(tp + d, TP)) for d in (2, 1, 3)]
    y_peers = [(lax.rem(y + d, RING) * 16 + z * 2 + c, tp) for d in (4, 3, 5, 2, 6, 1, 7)]
    z_peers = [(y * 16 + lax.rem(z + d, RING) * 2 + c, tp) for d in (4, 3, 5, 2, 6, 1, 7)]
    sibling = (y * 16 + z * 2 + (1 - c), tp)

    barrier = pltpu.get_barrier_semaphore()
    for peer in y_peers + z_peers + tp_peers + [sibling]:
        pl.semaphore_signal(barrier, inc=1, device_id=peer, device_id_type=MESH)
    loads[0].wait()
    pl.semaphore_wait(barrier, 18)

    def push(src, dst, stage, recv_sem, peer):
        pltpu.make_async_remote_copy(
            src, dst, sent.at[stage], recv_sem, device_id=peer, device_id_type=MESH
        ).start()

    def arrived(ref, sem):
        pltpu.make_async_copy(ref, ref, sem).wait()

    for i, peer in enumerate(tp_peers):
        push(gath.at[tp], gath.at[tp], 0, hsem.at[i], peer)
    loads[1].wait()

    def project(index, t):
        rows = pl.ds(pl.multiple_of(t * W, W), W)
        return jnp.dot(gath[t], wbuf[index, rows, :], preferred_element_type=F32)

    acc = project(0, tp)
    for i, d in ((1, 1), (2, 3), (0, 2)):
        t = lax.rem(tp + TP - d, TP)
        arrived(gath.at[t], hsem.at[i])
        acc = acc + project(0, t)
    query = acc.astype(BF16)

    column_head = iota((B, W), 1) // HD
    spread = jnp.concatenate(
        [jnp.where(column_head == h, query.astype(F32), 0.0) for h in range(4)], axis=0
    ).astype(BF16)
    row_b = iota((B, 1), 0)
    local_len = jnp.zeros((B, 1), jnp.int32)
    for b in range(B):
        local_len = jnp.where(row_b == b, lens[b] - seq * SPAN, local_len)
    low = jnp.concatenate([row_b * SPAN] * 4, axis=0)
    high = low + jnp.concatenate([jnp.clip(local_len, 0, SPAN)] * 4, axis=0)
    column = iota((4 * B, B * SPAN), 1)
    valid = jnp.logical_and(column >= low, column < high)
    loads[2].wait()
    keys = kbuf[...].reshape(B * SPAN, W)
    scores = lax.dot_general(spread, keys, (((1,), (1,)), ((), ())), preferred_element_type=F32)
    scores = jnp.where(valid, scores * HD ** (-0.5), NEG)
    top = jnp.max(scores, axis=1, keepdims=True)
    weights = jnp.where(valid, jnp.exp(scores - top), 0.0)
    total = jnp.sum(weights, axis=1, keepdims=True)
    loads[3].wait()
    summed = split_dot(weights, vbuf[...].reshape(B * SPAN, W))

    def fold(rows):
        result = jnp.broadcast_to(rows[0:B], (B, W))
        for h in range(1, 4):
            result = jnp.where(column_head == h, rows[h * B : (h + 1) * B], result)
        return result

    for core in range(2):
        for i, part in enumerate((fold(summed), fold(total), fold(top))):
            csend[core, i] = part[core * HALF : (core + 1) * HALF]
    push(csend.at[1 - c], crecv, 1, recv.at[0], sibling)

    loads[4].wait()
    new_key = sum(project(1, t) for t in range(TP)).astype(BF16)
    new_value = sum(project(2, t) for t in range(TP)).astype(BF16)

    arrived(crecv, recv.at[0])
    my_acc, my_total, my_top = csend[c, 0], csend[c, 1], csend[c, 2]
    both_top = jnp.maximum(my_top, crecv[2])
    mine, other = jnp.exp(my_top - both_top), jnp.exp(crecv[2] - both_top)
    both_acc = my_acc * mine + crecv[0] * other
    both_total = my_total * mine + crecv[1] * other

    def place(ref, slot, acc, row):
        base = pl.multiple_of(slot * SLOT, 8)
        ref[pl.ds(base, 8), :] = acc[:, :128]
        ref[pl.ds(base + 8, 8), :] = acc[:, 128:]
        ref[pl.ds(base + 16, 1), :] = row

    def slot_of(ref, slot, rows=SENT):
        return ref.at[pl.ds(pl.multiple_of(slot * SLOT, 8), rows), :]

    def wait_ring(ref, sem):
        arrived(ref.at[pl.ds(0, 7 * SENT), :], sem)

    def ring_acc(ref, factors):
        acc = None
        for s in range(RING):
            part = jnp.concatenate(
                [ref[s * SLOT : s * SLOT + 8, :], ref[s * SLOT + 8 : s * SLOT + 16, :]], axis=1
            ) * factors[s * 8 : s * 8 + 8]
            acc = part if acc is None else acc + part
        return acc

    place(yb, y, both_acc, to_row(both_top, both_total))
    for peer in y_peers:
        push(slot_of(yb, y), slot_of(yb, y), 2, recv.at[1], peer)

    same_head = iota((W, W), 0) // HD == iota((W, W), 1) // HD
    new_score = split_dot(
        query.astype(F32) * new_key.astype(F32), jnp.where(same_head, 1.0, 0.0).astype(BF16)
    ) * HD ** (-0.5)

    def own_half(rows):
        return jnp.where(c == 0, rows[:HALF], rows[HALF:])

    new_row = to_row(own_half(new_score), jnp.ones((HALF, W), F32))
    new_acc = own_half(new_value.astype(F32))
    position = iota((SPAN, W), 0)
    for b in range(B):
        hit = position == lens[b] - seq * SPAN
        kbuf[b] = jnp.where(hit, new_key[b : b + 1].astype(F32), kbuf[b].astype(F32)).astype(BF16)
        vbuf[b] = jnp.where(hit, new_value[b : b + 1].astype(F32), vbuf[b].astype(F32)).astype(BF16)
    stores = [
        pltpu.make_async_copy(kbuf, kout, lsem.at[2]),
        pltpu.make_async_copy(vbuf, vout, lsem.at[3]),
    ]
    for store in stores:
        store.start()

    wait_ring(yb, recv.at[1])
    max_lane = iota((1, 128), 1) % 16 < 8
    rows = yb[pl.ds(16, RING, stride=SLOT), :]
    ring_top = jnp.max(rows, axis=0, keepdims=True)
    factor = jnp.exp(rows - ring_top)
    ring_total = jnp.sum(rows * pltpu.roll(factor, 8, 1), axis=0, keepdims=True)
    place(zb, z, ring_acc(yb, spread_rows(factor)), jnp.where(max_lane, ring_top, ring_total))
    for peer in z_peers:
        push(slot_of(zb, z), slot_of(zb, z), 3, recv.at[2], peer)

    state = [own_half(gath[t].astype(F32)) for t in range(TP)]
    loads[5].wait()
    loads[6].wait()
    loads[7].wait()

    wait_ring(zb, recv.at[2])
    rows = zb[pl.ds(16, RING, stride=SLOT), :]
    last_top = jnp.maximum(jnp.max(rows, axis=0, keepdims=True), new_row)
    factor = jnp.exp(rows - last_top)
    new_factor = jnp.exp(new_row - last_top)
    last_total = jnp.sum(rows * pltpu.roll(factor, 8, 1), axis=0, keepdims=True)
    last_total = last_total + new_row * pltpu.roll(new_factor, 8, 1)
    share = pltpu.roll(last_total, 120, 1)
    factors = spread_rows(jnp.concatenate([factor / share, new_factor / share], axis=0))
    attended = ring_acc(zb, factors) + new_acc * factors[RING * 8 :]
    mixb[tp] = jnp.dot(attended.astype(BF16), wobuf[...], preferred_element_type=F32)
    for peer in tp_peers:
        push(mixb.at[tp], mixb.at[tp], 4, recv.at[3], peer)
    arrived(mixb.at[pl.ds(0, 3)], recv.at[3])
    resid = []
    for t in range(TP):
        lanes = slice(t * W, (t + 1) * W)
        resid.append(
            state[t] + ((mixb[0, :, lanes] + mixb[1, :, lanes]) + (mixb[2, :, lanes] + mixb[3, :, lanes]))
        )
    mean = jnp.sum((resid[0] + resid[1]) + (resid[2] + resid[3]), axis=1, keepdims=True) / D
    centred = [part - mean for part in resid]
    square = [part * part for part in centred]
    var = jnp.sum((square[0] + square[1]) + (square[2] + square[3]), axis=1, keepdims=True) / D
    own = centred[0]
    for t in range(1, TP):
        own = jnp.where(tp == t, centred[t], own)
    fin[c] = own / jnp.sqrt(var + 1e-05) * gbuf[...] + bbuf[...]
    push(fin.at[c], fin.at[c], 5, recv.at[4], sibling)

    for store in stores:
        store.wait()
    arrived(gath.at[pl.ds(0, 3)], sent.at[0])
    arrived(crecv, sent.at[1])
    wait_ring(yb, sent.at[2])
    wait_ring(zb, sent.at[3])
    arrived(mixb.at[pl.ds(0, 3)], sent.at[4])
    arrived(fin.at[0], recv.at[4])
    obuf[...] = jnp.concatenate([fin[0], fin[1]], axis=0).astype(BF16)
    last = pltpu.make_async_copy(obuf, out, lsem.at[0])
    last.start()
    arrived(fin.at[0], sent.at[5])
    last.wait()


def hand_out(o_in, k_in, v_in, o_out, k_out, v_out, obuf, kbuf, vbuf, sem):
    pairs = ((k_in, kbuf, k_out), (v_in, vbuf, v_out), (o_in, obuf, o_out))
    ins = [pltpu.make_async_copy(a, b, sem.at[i]) for i, (a, b, _) in enumerate(pairs)]
    outs = [pltpu.make_async_copy(b, d, sem.at[3 + i]) for i, (_, b, d) in enumerate(pairs)]
    for copy in ins:
        copy.start()
    for first, second in zip(ins, outs):
        first.wait()
        second.start()
    for copy in outs:
        copy.wait()


def body(hidden_in, w_qkv, w_out, key_cache, value_cache, lengths, ln_gain, ln_bias):
    hbm = pl.BlockSpec(memory_space=pl.ANY)
    cache = jax.ShapeDtypeStruct((B, SPAN, W), BF16)
    results = (jax.ShapeDtypeStruct((B, W), BF16), cache, cache)
    dma = pltpu.SemaphoreType.DMA
    done = pl.pallas_call(
        kernel,
        out_shape=results,
        in_specs=[pl.BlockSpec(memory_space=pltpu.SMEM)] + [hbm] * 7,
        out_specs=(hbm, hbm, hbm),
        scratch_shapes=[
            pltpu.VMEM((TP, B, W), BF16),
            pltpu.VMEM((3, D, W), BF16),
            pltpu.VMEM((W, D), BF16),
            pltpu.VMEM((B, SPAN, W), BF16),
            pltpu.VMEM((B, SPAN, W), BF16),
            pltpu.VMEM((1, W), F32),
            pltpu.VMEM((1, W), F32),
            pltpu.VMEM((2, 3, HALF, W), F32),
            pltpu.VMEM((3, HALF, W), F32),
            pltpu.VMEM((RING * SLOT, 128), F32),
            pltpu.VMEM((RING * SLOT, 128), F32),
            pltpu.VMEM((TP, HALF, D), F32),
            pltpu.VMEM((2, HALF, W), F32),
            pltpu.VMEM((B, W), BF16),
            dma((8,)), dma((3,)), dma((5,)), dma((6,)),
        ],
        compiler_params=pltpu.CompilerParams(collective_id=0, has_side_effects=True),
        name="sublayer",
    )(
        lengths, hidden_in, w_qkv, w_out, key_cache, value_cache,
        ln_gain.reshape(1, W), ln_bias.reshape(1, W),
    )
    return pl.pallas_call(
        hand_out,
        out_shape=results,
        in_specs=[hbm] * 3,
        out_specs=(hbm, hbm, hbm),
        scratch_shapes=[
            pltpu.VMEM((B, W), BF16),
            pltpu.VMEM((B, SPAN, W), BF16),
            pltpu.VMEM((B, SPAN, W), BF16),
            dma((6,)),
        ],
        name="hand_out",
    )(*done)


def solution(mesh):
    in_specs = (
        P(None, "tp"),
        P(None, None, "tp"),
        P("tp", None),
        P(None, "seq", "tp"),
        P(None, "seq", "tp"),
        P(),
        P("tp"),
        P("tp"),
    )
    out_specs = (P(None, "tp"), P(None, "seq", "tp"), P(None, "seq", "tp"))
    return jax.shard_map(body, mesh=mesh, in_specs=in_specs, out_specs=out_specs, check_vma=False)
```

time: 822 us -> 39.7 us (0.05)
  blocking collectives: 768 us -> 0 us
  Pallas kernels: 0 us -> 38.9 us
  waiting for transfers between devices: 21.1 us -> 0 us
  between operations: 14.1 us -> 0.64 us
    psum x3 -> x0, blocking collectives: 501 us -> none  [the longest x1 487 us: body(): total_all, summed_all = lax.psum((total_part, summed_part), 'seq')]
    pmax x1 -> x0, blocking collectives: 257 us -> none  [body(): top_all = lax.pmax(local_top, 'seq')]
    pallas_call x0 -> x2, Pallas kernels: none -> 38.9 us  [the longest x1 36.9 us: body(): pl.pallas_call(kernel, out_shape=results, in_specs=[pl.BlockSpec(memory_s...]
    reduce_scatter x1 -> x0, waiting for transfers between devices: 21.1 us -> none  [body(): lax.psum_scatter(lax.dot_general(w_out, attended, (((0,), (1,)), ((), ())...]
    all_gather x1 -> x0, blocking collectives: 10.5 us -> none  [body(): features = lax.all_gather(hidden_in, 'tp', axis=1, tiled=True)]
  transfers between devices with their start and end apart: 1 -> 0, of which waited for: 1 -> 0; matrix products, arithmetic and copies ran while one was open for 0% -> 0% of each run, Pallas kernels for 0% -> 0%
where the time goes in v2:
time: 39.7 us; the launch traced here: 39.6 us
  Pallas kernels  38.9 us (98%)
  between operations  0.64 us (2%)
    pallas_call x1, Pallas kernels, body(): pl.pallas_call(kernel, out_shape=results, in_specs=[pl.BlockSpec(memory_s...  36.9 us
    pallas_call x1, Pallas kernels, body(): pl.pallas_call(hand_out, out_shape=results, in_specs=[hbm] * 3, out_specs...  2.06 us

profile of v2, /device:TPU:1, one launch (start us, length us, event | category | flops | bytes accessed | tf_op | source)
XLA Modules:
  0.0 39.6 jit_solution(2937764563747507640)
XLA Ops:
  0.6 36.9 %sublayer.1 = (bf16[16,256]{1,0:T(8,128)(2,1)}, bf16[16,64,256]{2,1,0:T(8,128)(2,1)}, bf16[16,64,256]{2,1,0:T(8,128)(2,1)}) custom-call(s32[16]{0:T(128)} %lens.1, bf16[16,256]{1,0:T(8,128)(2,1)} %hid.1, bf16[3,1024,256]{2,1,0:T(8,128)(2,1)} %wqkv.1, bf16[256,1024]{1,0:T(8,128)(2,1)} %wout.1, bf16[16,64,256]{2,1,0:T(8,128)(2,1)} %kc.1, ...), custom_call_target="tpu_custom_call" | custom-call | tf_op jit(solution)/shard_map/sublayer/pallas_call | solution.py:281
  37.5 2.1 %hand_out.1 = (bf16[16,256]{1,0:T(8,128)(2,1)}, bf16[16,64,256]{2,1,0:T(8,128)(2,1)}, bf16[16,64,256]{2,1,0:T(8,128)(2,1)}) custom-call(bf16[16,256]{1,0:T(8,128)(2,1)} %get-tuple-element.6.o_in, bf16[16,64,256]{2,1,0:T(8,128)(2,1)} %get-tuple-element.7.k_in, bf16[16,64,256]{2,1,0:T(8,128)(2,1)} %get-tuple-element.8.v_in), custom_call_target="tpu_custom_call" | custom-call | tf_op jit(solution)/shard_map/hand_out/pallas_call | solution.py:309

commit v3 on v2

--- a/solution.py
+++ b/solution.py
@@ -52,10 +52,10 @@
 
 
 def kernel(
-    lens, hid, wqkv, wout, kc, vc, gain, bias,
-    out, kout, vout,
-    gath, wbuf, wobuf, kbuf, vbuf, gbuf, bbuf,
-    csend, crecv, yb, zb, mixb, fin, obuf,
+    lengths, hid, wqkv, wout, kc, vc, gain, bias,
+    out, kbuf, vbuf,
+    lens, gath, wbuf, wobuf, gbuf, bbuf,
+    csend, crecv, yb, zb, mixb, fin,
     lsem, hsem, recv, sent,
 ):
     seq = lax.axis_index("seq")
@@ -71,6 +71,7 @@
         pltpu.make_async_copy(wout, wobuf, lsem.at[5]),
         pltpu.make_async_copy(gain, gbuf, lsem.at[6]),
         pltpu.make_async_copy(bias, bbuf, lsem.at[7]),
+        pltpu.make_async_copy(lengths, lens, lsem.at[8]),
     ]
     for load in loads:
         load.start()
@@ -81,7 +82,7 @@
     sibling = (y * 16 + z * 2 + (1 - c), tp)
 
     barrier = pltpu.get_barrier_semaphore()
-    for peer in y_peers + z_peers + tp_peers + [sibling]:
+    for peer in tp_peers + [sibling] + y_peers + z_peers:
         pl.semaphore_signal(barrier, inc=1, device_id=peer, device_id_type=MESH)
     loads[0].wait()
     pl.semaphore_wait(barrier, 18)
@@ -114,6 +115,7 @@
         [jnp.where(column_head == h, query.astype(F32), 0.0) for h in range(4)], axis=0
     ).astype(BF16)
     row_b = iota((B, 1), 0)
+    loads[8].wait()
     local_len = jnp.zeros((B, 1), jnp.int32)
     for b in range(B):
         local_len = jnp.where(row_b == b, lens[b] - seq * SPAN, local_len)
@@ -193,13 +195,6 @@
         hit = position == lens[b] - seq * SPAN
         kbuf[b] = jnp.where(hit, new_key[b : b + 1].astype(F32), kbuf[b].astype(F32)).astype(BF16)
         vbuf[b] = jnp.where(hit, new_value[b : b + 1].astype(F32), vbuf[b].astype(F32)).astype(BF16)
-    stores = [
-        pltpu.make_async_copy(kbuf, kout, lsem.at[2]),
-        pltpu.make_async_copy(vbuf, vout, lsem.at[3]),
-    ]
-    for store in stores:
-        store.start()
-
     wait_ring(yb, recv.at[1])
     max_lane = iota((1, 128), 1) % 16 < 8
     rows = yb[pl.ds(16, RING, stride=SLOT), :]
@@ -245,50 +240,40 @@
     fin[c] = own / jnp.sqrt(var + 1e-05) * gbuf[...] + bbuf[...]
     push(fin.at[c], fin.at[c], 5, recv.at[4], sibling)
 
-    for store in stores:
-        store.wait()
     arrived(gath.at[pl.ds(0, 3)], sent.at[0])
     arrived(crecv, sent.at[1])
     wait_ring(yb, sent.at[2])
     wait_ring(zb, sent.at[3])
     arrived(mixb.at[pl.ds(0, 3)], sent.at[4])
     arrived(fin.at[0], recv.at[4])
-    obuf[...] = jnp.concatenate([fin[0], fin[1]], axis=0).astype(BF16)
-    last = pltpu.make_async_copy(obuf, out, lsem.at[0])
-    last.start()
+    out[...] = jnp.concatenate([fin[0], fin[1]], axis=0).astype(BF16)
     arrived(fin.at[0], sent.at[5])
-    last.wait()
-
-
-def hand_out(o_in, k_in, v_in, o_out, k_out, v_out, obuf, kbuf, vbuf, sem):
-    pairs = ((k_in, kbuf, k_out), (v_in, vbuf, v_out), (o_in, obuf, o_out))
-    ins = [pltpu.make_async_copy(a, b, sem.at[i]) for i, (a, b, _) in enumerate(pairs)]
-    outs = [pltpu.make_async_copy(b, d, sem.at[3 + i]) for i, (_, b, d) in enumerate(pairs)]
-    for copy in ins:
+
+
+def hand_out(o_in, k_in, v_in, o_out, k_out, v_out, sem):
+    pairs = ((k_in, k_out), (v_in, v_out), (o_in, o_out))
+    copies = [pltpu.make_async_copy(a, b, sem.at[i]) for i, (a, b) in enumerate(pairs)]
+    for copy in copies:
         copy.start()
-    for first, second in zip(ins, outs):
-        first.wait()
-        second.start()
-    for copy in outs:
+    for copy in copies:
         copy.wait()
 
 
 def body(hidden_in, w_qkv, w_out, key_cache, value_cache, lengths, ln_gain, ln_bias):
     hbm = pl.BlockSpec(memory_space=pl.ANY)
-    cache = jax.ShapeDtypeStruct((B, SPAN, W), BF16)
-    results = (jax.ShapeDtypeStruct((B, W), BF16), cache, cache)
+    vmem = pl.BlockSpec(memory_space=pltpu.VMEM)
+    cache = (B, SPAN, W)
     dma = pltpu.SemaphoreType.DMA
     done = pl.pallas_call(
         kernel,
-        out_shape=results,
-        in_specs=[pl.BlockSpec(memory_space=pltpu.SMEM)] + [hbm] * 7,
-        out_specs=(hbm, hbm, hbm),
+        out_shape=(pltpu.VMEM((B, W), BF16), pltpu.VMEM(cache, BF16), pltpu.VMEM(cache, BF16)),
+        in_specs=[hbm] * 8,
+        out_specs=(vmem, vmem, vmem),
         scratch_shapes=[
+            pltpu.SMEM((B,), jnp.int32),
             pltpu.VMEM((TP, B, W), BF16),
             pltpu.VMEM((3, D, W), BF16),
             pltpu.VMEM((W, D), BF16),
-            pltpu.VMEM((B, SPAN, W), BF16),
-            pltpu.VMEM((B, SPAN, W), BF16),
             pltpu.VMEM((1, W), F32),
             pltpu.VMEM((1, W), F32),
             pltpu.VMEM((2, 3, HALF, W), F32),
@@ -297,8 +282,7 @@
             pltpu.VMEM((RING * SLOT, 128), F32),
             pltpu.VMEM((TP, HALF, D), F32),
             pltpu.VMEM((2, HALF, W), F32),
-            pltpu.VMEM((B, W), BF16),
-            dma((8,)), dma((3,)), dma((5,)), dma((6,)),
+            dma((9,)), dma((3,)), dma((5,)), dma((6,)),
         ],
         compiler_params=pltpu.CompilerParams(collective_id=0, has_side_effects=True),
         name="sublayer",
@@ -308,17 +292,16 @@
     )
     return pl.pallas_call(
         hand_out,
-        out_shape=results,
-        in_specs=[hbm] * 3,
+        out_shape=(
+            jax.ShapeDtypeStruct((B, W), BF16),
+            jax.ShapeDtypeStruct(cache, BF16),
+            jax.ShapeDtypeStruct(cache, BF16),
+        ),
+        in_specs=[vmem] * 3,
         out_specs=(hbm, hbm, hbm),
-        scratch_shapes=[
-            pltpu.VMEM((B, W), BF16),
-            pltpu.VMEM((B, SPAN, W), BF16),
-            pltpu.VMEM((B, SPAN, W), BF16),
-            dma((6,)),
-        ],
+        scratch_shapes=[dma((3,))],
         name="hand_out",
-    )(*done)
+    )(*[pltpu.with_memory_space_constraint(part, pltpu.VMEM) for part in done])
 
 
 def solution(mesh):

time: 39.7 us -> 37.5 us (0.945)
  Pallas kernels: 38.9 us -> 36.7 us
    pallas_call x2, Pallas kernels: 38.9 us -> 36.7 us  [the longest x1 35.7 us: body(): pl.pallas_call(kernel, out_shape=(pltpu.VMEM((B, W), BF16), pltpu.VMEM(ca...]
where the time goes in v3:
time: 37.5 us; the launch traced here: 37.4 us
  Pallas kernels  36.7 us (98%)
  between operations  0.64 us (2%)
    pallas_call x1, Pallas kernels, body(): pl.pallas_call(kernel, out_shape=(pltpu.VMEM((B, W), BF16), pltpu.VMEM(ca...  35.7 us
    pallas_call x1, Pallas kernels, body(): pl.pallas_call(hand_out, out_shape=(jax.ShapeDtypeStruct((B, W), BF16), j...  1 us

profile of v3, /device:TPU:1, one launch (start us, length us, event | category | flops | bytes accessed | tf_op | source)
XLA Modules:
  0.0 37.4 jit_solution(18010692821240361184)
XLA Ops:
  0.6 35.7 %sublayer.1 = (bf16[16,256]{1,0:T(8,128)(2,1)S(1)}, bf16[16,64,256]{2,1,0:T(8,128)(2,1)S(1)}, bf16[16,64,256]{2,1,0:T(8,128)(2,1)S(1)}) custom-call(s32[16]{0:T(128)} %lengths.1, bf16[16,256]{1,0:T(8,128)(2,1)} %hid.1, bf16[3,1024,256]{2,1,0:T(8,128)(2,1)} %wqkv.1, bf16[256,1024]{1,0:T(8,128)(2,1)} %wout.1, bf16[16,64,256]{2,1,0:T(8,128)(2,1)} %kc.1, ...), custom_call_target="tpu_custom_call" | custom-call | tf_op jit(solution)/shard_map/sublayer/pallas_call | solution.py:267
  36.4 1.0 %hand_out.1 = (bf16[16,256]{1,0:T(8,128)(2,1)}, bf16[16,64,256]{2,1,0:T(8,128)(2,1)}, bf16[16,64,256]{2,1,0:T(8,128)(2,1)}) custom-call(bf16[16,256]{1,0:T(8,128)(2,1)S(1)} %get-tuple-element.6.o_in, bf16[16,64,256]{2,1,0:T(8,128)(2,1)S(1)} %get-tuple-element.7.k_in, bf16[16,64,256]{2,1,0:T(8,128)(2,1)S(1)} %get-tuple-element.8.v_in), custom_call_target="tpu_custom_call" | custom-call | tf_op jit(solution)/shard_map/hand_out/pallas_call | solution.py:293

commit v4 on v3

--- a/solution.py
+++ b/solution.py
@@ -54,38 +54,46 @@
 def kernel(
     lengths, hid, wqkv, wout, kc, vc, gain, bias,
     out, kbuf, vbuf,
-    lens, gath, wbuf, wobuf, gbuf, bbuf,
+    lens, gath, qkv, wbuf, wobuf, gbuf, bbuf,
     csend, crecv, yb, zb, mixb, fin,
-    lsem, hsem, recv, sent,
+    lsem, hsem, recv, sent, ready,
 ):
     seq = lax.axis_index("seq")
     tp = lax.axis_index("tp")
     y, z, c = seq // 16, (seq % 16) // 2, seq % 2
 
+    is_src = jnp.logical_or(z == 0, z == 3)
     loads = [
         pltpu.make_async_copy(hid, gath.at[tp], lsem.at[0]),
-        pltpu.make_async_copy(wqkv.at[0], wbuf.at[0], lsem.at[1]),
+        pltpu.make_async_copy(wqkv, wbuf, lsem.at[1]),
         pltpu.make_async_copy(kc, kbuf, lsem.at[2]),
         pltpu.make_async_copy(vc, vbuf, lsem.at[3]),
-        pltpu.make_async_copy(wqkv.at[pl.ds(1, 2)], wbuf.at[pl.ds(1, 2)], lsem.at[4]),
+        pltpu.make_async_copy(lengths, lens, lsem.at[4]),
         pltpu.make_async_copy(wout, wobuf, lsem.at[5]),
         pltpu.make_async_copy(gain, gbuf, lsem.at[6]),
         pltpu.make_async_copy(bias, bbuf, lsem.at[7]),
-        pltpu.make_async_copy(lengths, lens, lsem.at[8]),
     ]
-    for load in loads:
-        load.start()
+
+    def at_z(other):
+        return (y * 16 + other * 2 + c, tp)
 
     tp_peers = [(seq, lax.rem(tp + d, TP)) for d in (2, 1, 3)]
     y_peers = [(lax.rem(y + d, RING) * 16 + z * 2 + c, tp) for d in (4, 3, 5, 2, 6, 1, 7)]
-    z_peers = [(y * 16 + lax.rem(z + d, RING) * 2 + c, tp) for d in (4, 3, 5, 2, 6, 1, 7)]
+    z_peers = [at_z(lax.rem(z + d, RING)) for d in (4, 3, 5, 2, 6, 1, 7)]
     sibling = (y * 16 + z * 2 + (1 - c), tp)
 
+    step = jnp.where(z == 3, 1, RING - 1)
+    served = [
+        at_z(lax.rem(z + RING - step, RING)),
+        at_z(lax.rem(z + step, RING)),
+        at_z(lax.rem(z + 2 * step, RING)),
+    ]
+    my_src = jnp.where(jnp.logical_or(z == 1, z >= 6), 0, 3)
+    my_index = jnp.where(z <= 2, 0, jnp.where(jnp.logical_or(z == 4, z == 7), 1, 2))
+    def signal(sem, peer):
+        pl.semaphore_signal(sem, inc=1, device_id=peer, device_id_type=MESH)
+
     barrier = pltpu.get_barrier_semaphore()
-    for peer in tp_peers + [sibling] + y_peers + z_peers:
-        pl.semaphore_signal(barrier, inc=1, device_id=peer, device_id_type=MESH)
-    loads[0].wait()
-    pl.semaphore_wait(barrier, 18)
 
     def push(src, dst, stage, recv_sem, peer):
         pltpu.make_async_remote_copy(
@@ -95,27 +103,55 @@
     def arrived(ref, sem):
         pltpu.make_async_copy(ref, ref, sem).wait()
 
-    for i, peer in enumerate(tp_peers):
-        push(gath.at[tp], gath.at[tp], 0, hsem.at[i], peer)
-    loads[1].wait()
-
     def project(index, t):
         rows = pl.ds(pl.multiple_of(t * W, W), W)
         return jnp.dot(gath[t], wbuf[index, rows, :], preferred_element_type=F32)
 
-    acc = project(0, tp)
-    for i, d in ((1, 1), (2, 3), (0, 2)):
-        t = lax.rem(tp + TP - d, TP)
-        arrived(gath.at[t], hsem.at[i])
-        acc = acc + project(0, t)
-    query = acc.astype(BF16)
+    @pl.when(is_src)
+    def _():
+        for peer in tp_peers + [sibling, at_z(3 - z)] + y_peers:
+            signal(barrier, peer)
+        for load in loads:
+            load.start()
+        loads[0].wait()
+        pl.semaphore_wait(barrier, 12)
+        for i, peer in enumerate(tp_peers):
+            push(gath.at[tp], gath.at[tp], 0, hsem.at[i], peer)
+        for peer in served:
+            signal(barrier, peer)
+        loads[1].wait()
+        acc = [project(index, tp) for index in range(3)]
+        for i, d in ((1, 1), (2, 3), (0, 2)):
+            t = lax.rem(tp + TP - d, TP)
+            arrived(gath.at[t], hsem.at[i])
+            acc = [acc[index] + project(index, t) for index in range(3)]
+        for index in range(3):
+            qkv[index] = acc[index].astype(BF16)
+        for i in (1, 2, 0):
+            pl.semaphore_wait(ready.at[i], 1)
+            push(qkv.at[0], qkv.at[0], 6, recv.at[5], served[i])
+            push(qkv.at[pl.ds(1, 2)], qkv.at[pl.ds(1, 2)], 7, recv.at[6], served[i])
+        signal(ready.at[3], sibling)
+        for peer in y_peers + tp_peers + [at_z(3 - z)]:
+            signal(ready.at[4], peer)
+
+    @pl.when(jnp.logical_not(is_src))
+    def _():
+        pl.semaphore_wait(barrier, 1)
+        signal(ready.at[my_index], at_z(my_src))
+        for index, load in enumerate(loads):
+            if index != 1:
+                load.start()
+        arrived(qkv.at[0], recv.at[5])
+
+    query = qkv[0]
 
     column_head = iota((B, W), 1) // HD
     spread = jnp.concatenate(
         [jnp.where(column_head == h, query.astype(F32), 0.0) for h in range(4)], axis=0
     ).astype(BF16)
     row_b = iota((B, 1), 0)
-    loads[8].wait()
+    loads[4].wait()
     local_len = jnp.zeros((B, 1), jnp.int32)
     for b in range(B):
         local_len = jnp.where(row_b == b, lens[b] - seq * SPAN, local_len)
@@ -142,11 +178,18 @@
     for core in range(2):
         for i, part in enumerate((fold(summed), fold(total), fold(top))):
             csend[core, i] = part[core * HALF : (core + 1) * HALF]
+
+    @pl.when(is_src)
+    def _():
+        pl.semaphore_wait(ready.at[3], 1)
+        for peer in served:
+            signal(ready.at[5], peer)
+
+    @pl.when(jnp.logical_not(is_src))
+    def _():
+        pl.semaphore_wait(ready.at[5], 1)
+
     push(csend.at[1 - c], crecv, 1, recv.at[0], sibling)
-
-    loads[4].wait()
-    new_key = sum(project(1, t) for t in range(TP)).astype(BF16)
-    new_value = sum(project(2, t) for t in range(TP)).astype(BF16)
 
     arrived(crecv, recv.at[0])
     my_acc, my_total, my_top = csend[c, 0], csend[c, 1], csend[c, 2]
@@ -177,9 +220,26 @@
         return acc
 
     place(yb, y, both_acc, to_row(both_top, both_total))
+
+    @pl.when(is_src)
+    def _():
+        pl.semaphore_wait(ready.at[4], 11)
+        for peer in served:
+            signal(ready.at[6], peer)
+
+    @pl.when(jnp.logical_not(is_src))
+    def _():
+        pl.semaphore_wait(ready.at[6], 1)
+
     for peer in y_peers:
         push(slot_of(yb, y), slot_of(yb, y), 2, recv.at[1], peer)
 
+    @pl.when(jnp.logical_not(is_src))
+    def _():
+        loads[0].wait()
+        arrived(qkv.at[pl.ds(1, 2)], recv.at[6])
+
+    new_key, new_value = qkv[1], qkv[2]
     same_head = iota((W, W), 0) // HD == iota((W, W), 1) // HD
     new_score = split_dot(
         query.astype(F32) * new_key.astype(F32), jnp.where(same_head, 1.0, 0.0).astype(BF16)
@@ -205,7 +265,6 @@
     for peer in z_peers:
         push(slot_of(zb, z), slot_of(zb, z), 3, recv.at[2], peer)
 
-    state = [own_half(gath[t].astype(F32)) for t in range(TP)]
     loads[5].wait()
     loads[6].wait()
     loads[7].wait()
@@ -221,15 +280,15 @@
     factors = spread_rows(jnp.concatenate([factor / share, new_factor / share], axis=0))
     attended = ring_acc(zb, factors) + new_acc * factors[RING * 8 :]
     mixb[tp] = jnp.dot(attended.astype(BF16), wobuf[...], preferred_element_type=F32)
+    own_columns = pl.ds(pl.multiple_of(tp * W, W), W)
+    mixb[tp, :, own_columns] = mixb[tp, :, own_columns] + own_half(gath[tp].astype(F32))
     for peer in tp_peers:
         push(mixb.at[tp], mixb.at[tp], 4, recv.at[3], peer)
     arrived(mixb.at[pl.ds(0, 3)], recv.at[3])
     resid = []
     for t in range(TP):
         lanes = slice(t * W, (t + 1) * W)
-        resid.append(
-            state[t] + ((mixb[0, :, lanes] + mixb[1, :, lanes]) + (mixb[2, :, lanes] + mixb[3, :, lanes]))
-        )
+        resid.append((mixb[0, :, lanes] + mixb[1, :, lanes]) + (mixb[2, :, lanes] + mixb[3, :, lanes]))
     mean = jnp.sum((resid[0] + resid[1]) + (resid[2] + resid[3]), axis=1, keepdims=True) / D
     centred = [part - mean for part in resid]
     square = [part * part for part in centred]
@@ -240,7 +299,12 @@
     fin[c] = own / jnp.sqrt(var + 1e-05) * gbuf[...] + bbuf[...]
     push(fin.at[c], fin.at[c], 5, recv.at[4], sibling)
 
-    arrived(gath.at[pl.ds(0, 3)], sent.at[0])
+    @pl.when(is_src)
+    def _():
+        arrived(gath.at[pl.ds(0, 3)], sent.at[0])
+        arrived(qkv, sent.at[6])
+        arrived(wbuf.at[0, pl.ds(0, 6 * B), :], sent.at[7])
+
     arrived(crecv, sent.at[1])
     wait_ring(yb, sent.at[2])
     wait_ring(zb, sent.at[3])
@@ -272,6 +336,7 @@
         scratch_shapes=[
             pltpu.SMEM((B,), jnp.int32),
             pltpu.VMEM((TP, B, W), BF16),
+            pltpu.VMEM((3, B, W), BF16),
             pltpu.VMEM((3, D, W), BF16),
             pltpu.VMEM((W, D), BF16),
             pltpu.VMEM((1, W), F32),
@@ -282,7 +347,7 @@
             pltpu.VMEM((RING * SLOT, 128), F32),
             pltpu.VMEM((TP, HALF, D), F32),
             pltpu.VMEM((2, HALF, W), F32),
-            dma((9,)), dma((3,)), dma((5,)), dma((6,)),
+            dma((8,)), dma((3,)), dma((7,)), dma((8,)), pltpu.SemaphoreType.REGULAR((7,)),
         ],
         compiler_params=pltpu.CompilerParams(collective_id=0, has_side_effects=True),
         name="sublayer",

time: 37.5 us -> 39 us (1.040)
  Pallas kernels: 36.7 us -> 38.3 us
    pallas_call x1, Pallas kernels: 35.7 us -> 37.3 us  [body(): pl.pallas_call(kernel, out_shape=(pltpu.VMEM((B, W), BF16), pltpu.VMEM(ca...]
where the time goes in v4:
time: 39 us; the launch traced here: 38.9 us
  Pallas kernels  38.3 us (98%)
  between operations  0.64 us (2%)
    pallas_call x1, Pallas kernels, body(): pl.pallas_call(kernel, out_shape=(pltpu.VMEM((B, W), BF16), pltpu.VMEM(ca...  37.3 us
    pallas_call x1, Pallas kernels, body(): pl.pallas_call(hand_out, out_shape=(jax.ShapeDtypeStruct((B, W), BF16), j...  1 us

profile of v4, /device:TPU:1, one launch (start us, length us, event | category | flops | bytes accessed | tf_op | source)
XLA Modules:
  0.0 38.9 jit_solution(5973308887953143095)
XLA Ops:
  0.6 37.3 %sublayer.1 = (bf16[16,256]{1,0:T(8,128)(2,1)S(1)}, bf16[16,64,256]{2,1,0:T(8,128)(2,1)S(1)}, bf16[16,64,256]{2,1,0:T(8,128)(2,1)S(1)}) custom-call(s32[16]{0:T(128)} %lengths.1, bf16[16,256]{1,0:T(8,128)(2,1)} %hid.1, bf16[3,1024,256]{2,1,0:T(8,128)(2,1)} %wqkv.1, bf16[256,1024]{1,0:T(8,128)(2,1)} %wout.1, bf16[16,64,256]{2,1,0:T(8,128)(2,1)} %kc.1, ...), custom_call_target="tpu_custom_call" | custom-call | tf_op jit(solution)/shard_map/sublayer/pallas_call | solution.py:331
  37.9 1.0 %hand_out.1 = (bf16[16,256]{1,0:T(8,128)(2,1)}, bf16[16,64,256]{2,1,0:T(8,128)(2,1)}, bf16[16,64,256]{2,1,0:T(8,128)(2,1)}) custom-call(bf16[16,256]{1,0:T(8,128)(2,1)S(1)} %get-tuple-element.6.o_in, bf16[16,64,256]{2,1,0:T(8,128)(2,1)S(1)} %get-tuple-element.7.k_in, bf16[16,64,256]{2,1,0:T(8,128)(2,1)S(1)} %get-tuple-element.8.v_in), custom_call_target="tpu_custom_call" | custom-call | tf_op jit(solution)/shard_map/hand_out/pallas_call | solution.py:358

commit v5 on v3

--- a/solution.py
+++ b/solution.py
@@ -13,8 +13,8 @@
 TP = 4
 RING = 8
 SPAN = 64
-SLOT = 24
-SENT = 17
+SLOT = 16
+SENT = 9
 NEG = -1e30
 F32 = jnp.float32
 BF16 = jnp.bfloat16
@@ -36,19 +36,7 @@
     lane, request = iota((HALF, W), 1) % HD, iota((HALF, W), 0)
     picked = jnp.where(lane == request, tops, jnp.where(lane == request + HALF, totals, 0.0))
     row = jnp.sum(picked, axis=0, keepdims=True)
-    return row[:, :128] + pltpu.roll(row[:, 128:], 16, 1)
-
-
-def spread_rows(rows):
-    entry = iota((HALF, 128), 1)
-    keep = jnp.logical_and(entry % 16 == iota((HALF, 128), 0), entry % 64 < 32)
-    picked = jnp.concatenate(
-        [jnp.where(keep, rows[s : s + 1], 0.0) for s in range(rows.shape[0])], axis=0
-    )
-    lane, column = iota((128, W), 0), iota((128, W), 1)
-    head = lane // 64 + 2 * ((lane % 64) // 16)
-    matrix = jnp.where(jnp.logical_and(lane % 64 < 32, head == column // HD), 1.0, 0.0).astype(BF16)
-    return split_dot(picked, matrix)
+    return row[:, :128], row[:, 128:]
 
 
 def kernel(
@@ -103,6 +91,19 @@
         rows = pl.ds(pl.multiple_of(t * W, W), W)
         return jnp.dot(gath[t], wbuf[index, rows, :], preferred_element_type=F32)
 
+    column_head = iota((B, W), 1) // HD
+    row_b = iota((B, 1), 0)
+    loads[8].wait()
+    local_len = jnp.zeros((B, 1), jnp.int32)
+    for b in range(B):
+        local_len = jnp.where(row_b == b, lens[b] - seq * SPAN, local_len)
+    row_len = jnp.concatenate([local_len] * 4, axis=0)
+    request = iota((4 * B, 128), 0) % B
+    lane = iota((4 * B, 128), 1)
+    valid = jnp.logical_and(lane // SPAN == request % 2, lane % SPAN < row_len)
+    pair = request // 2
+    same_head = jnp.where(iota((128, 128), 0) // HD == iota((128, 128), 1) // HD, 1.0, 0.0).astype(BF16)
+
     acc = project(0, tp)
     for i, d in ((1, 1), (2, 3), (0, 2)):
         t = lax.rem(tp + TP - d, TP)
@@ -110,28 +111,31 @@
         acc = acc + project(0, t)
     query = acc.astype(BF16)
 
-    column_head = iota((B, W), 1) // HD
     spread = jnp.concatenate(
         [jnp.where(column_head == h, query.astype(F32), 0.0) for h in range(4)], axis=0
     ).astype(BF16)
-    row_b = iota((B, 1), 0)
-    loads[8].wait()
-    local_len = jnp.zeros((B, 1), jnp.int32)
-    for b in range(B):
-        local_len = jnp.where(row_b == b, lens[b] - seq * SPAN, local_len)
-    low = jnp.concatenate([row_b * SPAN] * 4, axis=0)
-    high = low + jnp.concatenate([jnp.clip(local_len, 0, SPAN)] * 4, axis=0)
-    column = iota((4 * B, B * SPAN), 1)
-    valid = jnp.logical_and(column >= low, column < high)
     loads[2].wait()
     keys = kbuf[...].reshape(B * SPAN, W)
-    scores = lax.dot_general(spread, keys, (((1,), (1,)), ((), ())), preferred_element_type=F32)
+    every = lax.dot_general(spread, keys, (((1,), (1,)), ((), ())), preferred_element_type=F32)
+    scores = every[:, :128]
+    for j in range(1, 8):
+        scores = jnp.where(pair == j, every[:, j * 128 : j * 128 + 128], scores)
     scores = jnp.where(valid, scores * HD ** (-0.5), NEG)
     top = jnp.max(scores, axis=1, keepdims=True)
     weights = jnp.where(valid, jnp.exp(scores - top), 0.0)
     total = jnp.sum(weights, axis=1, keepdims=True)
+    upper = weights.astype(BF16).astype(F32)
+    lower = weights - upper
+    wide = jnp.concatenate(
+        [
+            jnp.concatenate([jnp.where(pair == j, part, 0.0).astype(BF16) for j in range(8)], axis=1)
+            for part in (upper, lower)
+        ],
+        axis=0,
+    )
     loads[3].wait()
-    summed = split_dot(weights, vbuf[...].reshape(B * SPAN, W))
+    both = jnp.dot(wide, vbuf[...].reshape(B * SPAN, W), preferred_element_type=F32)
+    summed = both[: 4 * B] + both[4 * B :]
 
     def fold(rows):
         result = jnp.broadcast_to(rows[0:B], (B, W))
@@ -157,53 +161,71 @@
 
     def place(ref, slot, acc, row):
         base = pl.multiple_of(slot * SLOT, 8)
-        ref[pl.ds(base, 8), :] = acc[:, :128]
-        ref[pl.ds(base + 8, 8), :] = acc[:, 128:]
-        ref[pl.ds(base + 16, 1), :] = row
-
-    def slot_of(ref, slot, rows=SENT):
-        return ref.at[pl.ds(pl.multiple_of(slot * SLOT, 8), rows), :]
+        ref[pl.ds(base, 8), :] = acc
+        ref[pl.ds(base + 8, 1), :] = row
+
+    def slot_of(ref, slot):
+        return ref.at[pl.ds(pl.multiple_of(slot * SLOT, 8), SENT), :]
 
     def wait_ring(ref, sem):
-        arrived(ref.at[pl.ds(0, 7 * SENT), :], sem)
-
-    def ring_acc(ref, factors):
+        arrived(ref.at[pl.ds(0, 14 * SENT), :], sem)
+
+    def push_ring(ref, slot_y, slot_z, stage, recv_sem):
+        for y_peer, z_peer in zip(y_peers, z_peers):
+            push(slot_of(ref, slot_y), slot_of(ref, slot_y), stage, recv_sem, y_peer)
+            push(slot_of(ref, slot_z), slot_of(ref, slot_z), stage, recv_sem, z_peer)
+
+    def spread_rows(rows):
+        keep = iota((HALF, 128), 1) % HD == iota((HALF, 128), 0)
+        return split_dot(
+            jnp.concatenate(
+                [jnp.where(keep, rows[s : s + 1], 0.0) for s in range(rows.shape[0])], axis=0
+            ),
+            same_head,
+        )
+
+    def ring_acc(ref, factors, first):
         acc = None
-        for s in range(RING):
-            part = jnp.concatenate(
-                [ref[s * SLOT : s * SLOT + 8, :], ref[s * SLOT + 8 : s * SLOT + 16, :]], axis=1
-            ) * factors[s * 8 : s * 8 + 8]
+        for s in range(first, first + RING):
+            part = ref[s * SLOT : s * SLOT + 8, :] * factors[s * 8 : s * 8 + 8]
             acc = part if acc is None else acc + part
         return acc
 
-    place(yb, y, both_acc, to_row(both_top, both_total))
-    for peer in y_peers:
-        push(slot_of(yb, y), slot_of(yb, y), 2, recv.at[1], peer)
-
-    same_head = iota((W, W), 0) // HD == iota((W, W), 1) // HD
-    new_score = split_dot(
-        query.astype(F32) * new_key.astype(F32), jnp.where(same_head, 1.0, 0.0).astype(BF16)
-    ) * HD ** (-0.5)
+    def over(first, second):
+        return jnp.where(iota((2 * RING, 128), 0) < RING, first, second)
+
+    low_row, high_row = to_row(both_top, both_total)
+    place(yb, y, both_acc[:, :128], low_row)
+    place(yb, RING + z, both_acc[:, 128:], high_row)
+    push_ring(yb, y, RING + z, 2, recv.at[1])
+
+    product = query.astype(F32) * new_key.astype(F32)
+    halves = split_dot(jnp.concatenate([product[:, :128], product[:, 128:]], axis=0), same_head)
+    new_score = jnp.concatenate([halves[:B], halves[B:]], axis=1) * HD ** (-0.5)
 
     def own_half(rows):
         return jnp.where(c == 0, rows[:HALF], rows[HALF:])
 
-    new_row = to_row(own_half(new_score), jnp.ones((HALF, W), F32))
+    new_low, new_high = to_row(own_half(new_score), jnp.ones((HALF, W), F32))
     new_acc = own_half(new_value.astype(F32))
     position = iota((SPAN, W), 0)
     for b in range(B):
         hit = position == lens[b] - seq * SPAN
         kbuf[b] = jnp.where(hit, new_key[b : b + 1].astype(F32), kbuf[b].astype(F32)).astype(BF16)
         vbuf[b] = jnp.where(hit, new_value[b : b + 1].astype(F32), vbuf[b].astype(F32)).astype(BF16)
+    max_lane = iota((1, 128), 1) % HD < HALF
     wait_ring(yb, recv.at[1])
-    max_lane = iota((1, 128), 1) % 16 < 8
-    rows = yb[pl.ds(16, RING, stride=SLOT), :]
-    ring_top = jnp.max(rows, axis=0, keepdims=True)
-    factor = jnp.exp(rows - ring_top)
-    ring_total = jnp.sum(rows * pltpu.roll(factor, 8, 1), axis=0, keepdims=True)
-    place(zb, z, ring_acc(yb, spread_rows(factor)), jnp.where(max_lane, ring_top, ring_total))
-    for peer in z_peers:
-        push(slot_of(zb, z), slot_of(zb, z), 3, recv.at[2], peer)
+    rows = yb[pl.ds(8, 2 * RING, stride=SLOT), :]
+    low_top = jnp.max(rows[:RING], axis=0, keepdims=True)
+    high_top = jnp.max(rows[RING:], axis=0, keepdims=True)
+    factor = jnp.exp(rows - over(low_top, high_top))
+    totals = rows * pltpu.roll(factor, HALF, 1)
+    low_total = jnp.sum(totals[:RING], axis=0, keepdims=True)
+    high_total = jnp.sum(totals[RING:], axis=0, keepdims=True)
+    factors = spread_rows(factor)
+    place(zb, z, ring_acc(yb, factors, 0), jnp.where(max_lane, low_top, low_total))
+    place(zb, RING + y, ring_acc(yb, factors, RING), jnp.where(max_lane, high_top, high_total))
+    push_ring(zb, RING + y, z, 3, recv.at[2])
 
     state = [own_half(gath[t].astype(F32)) for t in range(TP)]
     loads[5].wait()
@@ -211,15 +233,27 @@
     loads[7].wait()
 
     wait_ring(zb, recv.at[2])
-    rows = zb[pl.ds(16, RING, stride=SLOT), :]
-    last_top = jnp.maximum(jnp.max(rows, axis=0, keepdims=True), new_row)
-    factor = jnp.exp(rows - last_top)
-    new_factor = jnp.exp(new_row - last_top)
-    last_total = jnp.sum(rows * pltpu.roll(factor, 8, 1), axis=0, keepdims=True)
-    last_total = last_total + new_row * pltpu.roll(new_factor, 8, 1)
-    share = pltpu.roll(last_total, 120, 1)
-    factors = spread_rows(jnp.concatenate([factor / share, new_factor / share], axis=0))
-    attended = ring_acc(zb, factors) + new_acc * factors[RING * 8 :]
+    rows = zb[pl.ds(8, 2 * RING, stride=SLOT), :]
+    low_top = jnp.maximum(jnp.max(rows[:RING], axis=0, keepdims=True), new_low)
+    high_top = jnp.maximum(jnp.max(rows[RING:], axis=0, keepdims=True), new_high)
+    factor = jnp.exp(rows - over(low_top, high_top))
+    totals = rows * pltpu.roll(factor, HALF, 1)
+    low_new, high_new = jnp.exp(new_low - low_top), jnp.exp(new_high - high_top)
+    low_total = jnp.sum(totals[:RING], axis=0, keepdims=True) + new_low * pltpu.roll(low_new, HALF, 1)
+    high_total = jnp.sum(totals[RING:], axis=0, keepdims=True) + new_high * pltpu.roll(high_new, HALF, 1)
+    low_share, high_share = pltpu.roll(low_total, 128 - HALF, 1), pltpu.roll(high_total, 128 - HALF, 1)
+    factors = spread_rows(
+        jnp.concatenate(
+            [factor / over(low_share, high_share), low_new / low_share, high_new / high_share], axis=0
+        )
+    )
+    attended = jnp.concatenate(
+        [
+            ring_acc(zb, factors, 0) + new_acc[:, :128] * factors[128:136],
+            ring_acc(zb, factors, RING) + new_acc[:, 128:] * factors[136:144],
+        ],
+        axis=1,
+    )
     mixb[tp] = jnp.dot(attended.astype(BF16), wobuf[...], preferred_element_type=F32)
     for peer in tp_peers:
         push(mixb.at[tp], mixb.at[tp], 4, recv.at[3], peer)
@@ -278,8 +312,8 @@
             pltpu.VMEM((1, W), F32),
             pltpu.VMEM((2, 3, HALF, W), F32),
             pltpu.VMEM((3, HALF, W), F32),
-            pltpu.VMEM((RING * SLOT, 128), F32),
-            pltpu.VMEM((RING * SLOT, 128), F32),
+            pltpu.VMEM((2 * RING * SLOT, 128), F32),
+            pltpu.VMEM((2 * RING * SLOT, 128), F32),
             pltpu.VMEM((TP, HALF, D), F32),
             pltpu.VMEM((2, HALF, W), F32),
             dma((9,)), dma((3,)), dma((5,)), dma((6,)),

time: 37.5 us -> 36.6 us (0.976)
  Pallas kernels: 36.7 us -> 35.9 us
    pallas_call x1, Pallas kernels: 35.7 us -> 34.9 us  [body(): pl.pallas_call(kernel, out_shape=(pltpu.VMEM((B, W), BF16), pltpu.VMEM(ca...]
where the time goes in v5:
time: 36.6 us; the launch traced here: 36.5 us
  Pallas kernels  35.9 us (98%)
  between operations  0.64 us (2%)
    pallas_call x1, Pallas kernels, body(): pl.pallas_call(kernel, out_shape=(pltpu.VMEM((B, W), BF16), pltpu.VMEM(ca...  34.9 us
    pallas_call x1, Pallas kernels, body(): pl.pallas_call(hand_out, out_shape=(jax.ShapeDtypeStruct((B, W), BF16), j...  1 us

profile of v5, /device:TPU:1, one launch (start us, length us, event | category | flops | bytes accessed | tf_op | source)
XLA Modules:
  0.0 36.5 jit_solution(3264549461975030581)
XLA Ops:
  0.6 34.9 %sublayer.1 = (bf16[16,256]{1,0:T(8,128)(2,1)S(1)}, bf16[16,64,256]{2,1,0:T(8,128)(2,1)S(1)}, bf16[16,64,256]{2,1,0:T(8,128)(2,1)S(1)}) custom-call(s32[16]{0:T(128)} %lengths.1, bf16[16,256]{1,0:T(8,128)(2,1)} %hid.1, bf16[3,1024,256]{2,1,0:T(8,128)(2,1)} %wqkv.1, bf16[256,1024]{1,0:T(8,128)(2,1)} %wout.1, bf16[16,64,256]{2,1,0:T(8,128)(2,1)} %kc.1, ...), custom_call_target="tpu_custom_call" | custom-call | tf_op jit(solution)/shard_map/sublayer/pallas_call | solution.py:301
  35.5 1.0 %hand_out.1 = (bf16[16,256]{1,0:T(8,128)(2,1)}, bf16[16,64,256]{2,1,0:T(8,128)(2,1)}, bf16[16,64,256]{2,1,0:T(8,128)(2,1)}) custom-call(bf16[16,256]{1,0:T(8,128)(2,1)S(1)} %get-tuple-element.6.o_in, bf16[16,64,256]{2,1,0:T(8,128)(2,1)S(1)} %get-tuple-element.7.k_in, bf16[16,64,256]{2,1,0:T(8,128)(2,1)S(1)} %get-tuple-element.8.v_in), custom_call_target="tpu_custom_call" | custom-call | tf_op jit(solution)/shard_map/hand_out/pallas_call | solution.py:327

commit v6 on v5

--- a/solution.py
+++ b/solution.py
@@ -42,7 +42,7 @@
 def kernel(
     lengths, hid, wqkv, wout, kc, vc, gain, bias,
     out, kbuf, vbuf,
-    lens, gath, wbuf, wobuf, gbuf, bbuf,
+    lens, gath, qkv, wbuf, wobuf, gbuf, bbuf,
     csend, crecv, yb, zb, mixb, fin,
     lsem, hsem, recv, sent,
 ):
@@ -61,17 +61,32 @@
         pltpu.make_async_copy(bias, bbuf, lsem.at[7]),
         pltpu.make_async_copy(lengths, lens, lsem.at[8]),
     ]
-    for load in loads:
-        load.start()
-
     tp_peers = [(seq, lax.rem(tp + d, TP)) for d in (2, 1, 3)]
     y_peers = [(lax.rem(y + d, RING) * 16 + z * 2 + c, tp) for d in (4, 3, 5, 2, 6, 1, 7)]
     z_peers = [(y * 16 + lax.rem(z + d, RING) * 2 + c, tp) for d in (4, 3, 5, 2, 6, 1, 7)]
     sibling = (y * 16 + z * 2 + (1 - c), tp)
 
     barrier = pltpu.get_barrier_semaphore()
-    for peer in tp_peers + [sibling] + y_peers + z_peers:
+    def signal(peer):
         pl.semaphore_signal(barrier, inc=1, device_id=peer, device_id_type=MESH)
+
+    for peer in tp_peers:
+        signal(peer)
+    loads[0].start()
+    for peer in [sibling] + z_peers + y_peers:
+        signal(peer)
+
+    @pl.when(c == 1)
+    def _():
+        loads[1].start()
+
+    for index in (8, 2, 3, 5, 6, 7):
+        loads[index].start()
+
+    @pl.when(c == 1)
+    def _():
+        loads[4].start()
+
     loads[0].wait()
     pl.semaphore_wait(barrier, 18)
 
@@ -83,13 +98,14 @@
     def arrived(ref, sem):
         pltpu.make_async_copy(ref, ref, sem).wait()
 
-    for i, peer in enumerate(tp_peers):
-        push(gath.at[tp], gath.at[tp], 0, hsem.at[i], peer)
-    loads[1].wait()
-
     def project(index, t):
         rows = pl.ds(pl.multiple_of(t * W, W), W)
         return jnp.dot(gath[t], wbuf[index, rows, :], preferred_element_type=F32)
+
+    @pl.when(c == 1)
+    def _():
+        for i, peer in enumerate(tp_peers):
+            push(gath.at[tp], gath.at[tp], 0, hsem.at[i], peer)
 
     column_head = iota((B, W), 1) // HD
     row_b = iota((B, 1), 0)
@@ -104,12 +120,22 @@
     pair = request // 2
     same_head = jnp.where(iota((128, 128), 0) // HD == iota((128, 128), 1) // HD, 1.0, 0.0).astype(BF16)
 
-    acc = project(0, tp)
-    for i, d in ((1, 1), (2, 3), (0, 2)):
-        t = lax.rem(tp + TP - d, TP)
-        arrived(gath.at[t], hsem.at[i])
-        acc = acc + project(0, t)
-    query = acc.astype(BF16)
+    @pl.when(c == 1)
+    def _():
+        loads[1].wait()
+        acc = project(0, tp)
+        for i, d in ((1, 1), (2, 3), (0, 2)):
+            t = lax.rem(tp + TP - d, TP)
+            arrived(gath.at[t], hsem.at[i])
+            acc = acc + project(0, t)
+        qkv[0] = acc.astype(BF16)
+        push(qkv.at[0], qkv.at[0], 6, recv.at[5], sibling)
+
+    @pl.when(c == 0)
+    def _():
+        arrived(qkv.at[0], recv.at[5])
+
+    query = qkv[0]
 
     spread = jnp.concatenate(
         [jnp.where(column_head == h, query.astype(F32), 0.0) for h in range(4)], axis=0
@@ -148,9 +174,12 @@
             csend[core, i] = part[core * HALF : (core + 1) * HALF]
     push(csend.at[1 - c], crecv, 1, recv.at[0], sibling)
 
-    loads[4].wait()
-    new_key = sum(project(1, t) for t in range(TP)).astype(BF16)
-    new_value = sum(project(2, t) for t in range(TP)).astype(BF16)
+    @pl.when(c == 1)
+    def _():
+        loads[4].wait()
+        for index in (1, 2):
+            qkv[index] = sum(project(index, t) for t in range(TP)).astype(BF16)
+        push(qkv.at[pl.ds(1, 2)], qkv.at[pl.ds(1, 2)], 7, recv.at[6], sibling)
 
     arrived(crecv, recv.at[0])
     my_acc, my_total, my_top = csend[c, 0], csend[c, 1], csend[c, 2]
@@ -199,6 +228,11 @@
     place(yb, RING + z, both_acc[:, 128:], high_row)
     push_ring(yb, y, RING + z, 2, recv.at[1])
 
+    @pl.when(c == 0)
+    def _():
+        arrived(qkv.at[pl.ds(1, 2)], recv.at[6])
+
+    new_key, new_value = qkv[1], qkv[2]
     product = query.astype(F32) * new_key.astype(F32)
     halves = split_dot(jnp.concatenate([product[:, :128], product[:, 128:]], axis=0), same_head)
     new_score = jnp.concatenate([halves[:B], halves[B:]], axis=1) * HD ** (-0.5)
@@ -227,7 +261,7 @@
     place(zb, RING + y, ring_acc(yb, factors, RING), jnp.where(max_lane, high_top, high_total))
     push_ring(zb, RING + y, z, 3, recv.at[2])
 
-    state = [own_half(gath[t].astype(F32)) for t in range(TP)]
+    own_hidden = own_half(gath[tp].astype(F32))
     loads[5].wait()
     loads[6].wait()
     loads[7].wait()
@@ -254,16 +288,20 @@
         ],
         axis=1,
     )
-    mixb[tp] = jnp.dot(attended.astype(BF16), wobuf[...], preferred_element_type=F32)
-    for peer in tp_peers:
-        push(mixb.at[tp], mixb.at[tp], 4, recv.at[3], peer)
+    attended = attended.astype(BF16)
+    for half in range(2):
+        lanes = slice(half * 2 * W, (half + 1) * 2 * W)
+        mixed = jnp.dot(attended, wobuf[:, lanes], preferred_element_type=F32)
+        for t in (2 * half, 2 * half + 1):
+            part = mixed[:, t % 2 * W : (t % 2 + 1) * W]
+            mixb[tp, :, t * W : (t + 1) * W] = part + jnp.where(tp == t, own_hidden, 0.0)
+        for peer in tp_peers:
+            push(mixb.at[tp, :, pl.ds(half * 2 * W, 2 * W)], mixb.at[tp, :, pl.ds(half * 2 * W, 2 * W)], 4, recv.at[3], peer)
     arrived(mixb.at[pl.ds(0, 3)], recv.at[3])
     resid = []
     for t in range(TP):
         lanes = slice(t * W, (t + 1) * W)
-        resid.append(
-            state[t] + ((mixb[0, :, lanes] + mixb[1, :, lanes]) + (mixb[2, :, lanes] + mixb[3, :, lanes]))
-        )
+        resid.append((mixb[0, :, lanes] + mixb[1, :, lanes]) + (mixb[2, :, lanes] + mixb[3, :, lanes]))
     mean = jnp.sum((resid[0] + resid[1]) + (resid[2] + resid[3]), axis=1, keepdims=True) / D
     centred = [part - mean for part in resid]
     square = [part * part for part in centred]
@@ -274,7 +312,12 @@
     fin[c] = own / jnp.sqrt(var + 1e-05) * gbuf[...] + bbuf[...]
     push(fin.at[c], fin.at[c], 5, recv.at[4], sibling)
 
-    arrived(gath.at[pl.ds(0, 3)], sent.at[0])
+    @pl.when(c == 1)
+    def _():
+        arrived(gath.at[pl.ds(0, 3)], sent.at[0])
+        arrived(qkv.at[0], sent.at[6])
+        arrived(qkv.at[pl.ds(1, 2)], sent.at[7])
+
     arrived(crecv, sent.at[1])
     wait_ring(yb, sent.at[2])
     wait_ring(zb, sent.at[3])
@@ -306,6 +349,7 @@
         scratch_shapes=[
             pltpu.SMEM((B,), jnp.int32),
             pltpu.VMEM((TP, B, W), BF16),
+            pltpu.VMEM((3, B, W), BF16),
             pltpu.VMEM((3, D, W), BF16),
             pltpu.VMEM((W, D), BF16),
             pltpu.VMEM((1, W), F32),
@@ -316,7 +360,7 @@
             pltpu.VMEM((2 * RING * SLOT, 128), F32),
             pltpu.VMEM((TP, HALF, D), F32),
             pltpu.VMEM((2, HALF, W), F32),
-            dma((9,)), dma((3,)), dma((5,)), dma((6,)),
+            dma((9,)), dma((3,)), dma((7,)), dma((8,)),
         ],
         compiler_params=pltpu.CompilerParams(collective_id=0, has_side_effects=True),
         name="sublayer",

time: 36.6 us -> 35.7 us (0.975)
  Pallas kernels: 35.9 us -> 34.9 us
    pallas_call x1, Pallas kernels: 34.9 us -> 33.9 us  [body(): pl.pallas_call(kernel, out_shape=(pltpu.VMEM((B, W), BF16), pltpu.VMEM(ca...]
where the time goes in v6:
time: 35.7 us; the launch traced here: 35.6 us
  Pallas kernels  34.9 us (98%)
  between operations  0.64 us (2%)
    pallas_call x1, Pallas kernels, body(): pl.pallas_call(kernel, out_shape=(pltpu.VMEM((B, W), BF16), pltpu.VMEM(ca...  33.9 us
    pallas_call x1, Pallas kernels, body(): pl.pallas_call(hand_out, out_shape=(jax.ShapeDtypeStruct((B, W), BF16), j...  1 us

profile of v6, /device:TPU:1, one launch (start us, length us, event | category | flops | bytes accessed | tf_op | source)
XLA Modules:
  0.0 35.6 jit_solution(6910210446964385679)
XLA Ops:
  0.6 33.9 %sublayer.1 = (bf16[16,256]{1,0:T(8,128)(2,1)S(1)}, bf16[16,64,256]{2,1,0:T(8,128)(2,1)S(1)}, bf16[16,64,256]{2,1,0:T(8,128)(2,1)S(1)}) custom-call(s32[16]{0:T(128)} %lengths.1, bf16[16,256]{1,0:T(8,128)(2,1)} %hid.1, bf16[3,1024,256]{2,1,0:T(8,128)(2,1)} %wqkv.1, bf16[256,1024]{1,0:T(8,128)(2,1)} %wout.1, bf16[16,64,256]{2,1,0:T(8,128)(2,1)} %kc.1, ...), custom_call_target="tpu_custom_call" | custom-call | tf_op jit(solution)/shard_map/sublayer/pallas_call | solution.py:344
  34.6 1.0 %hand_out.1 = (bf16[16,256]{1,0:T(8,128)(2,1)}, bf16[16,64,256]{2,1,0:T(8,128)(2,1)}, bf16[16,64,256]{2,1,0:T(8,128)(2,1)}) custom-call(bf16[16,256]{1,0:T(8,128)(2,1)S(1)} %get-tuple-element.6.o_in, bf16[16,64,256]{2,1,0:T(8,128)(2,1)S(1)} %get-tuple-element.7.k_in, bf16[16,64,256]{2,1,0:T(8,128)(2,1)S(1)} %get-tuple-element.8.v_in), custom_call_target="tpu_custom_call" | custom-call | tf_op jit(solution)/shard_map/hand_out/pallas_call | solution.py:371

commit v7 on v6

--- a/solution.py
+++ b/solution.py
@@ -44,7 +44,7 @@
     out, kbuf, vbuf,
     lens, gath, qkv, wbuf, wobuf, gbuf, bbuf,
     csend, crecv, yb, zb, mixb, fin,
-    lsem, hsem, recv, sent,
+    lsem, hsem, recv, sent, ready,
 ):
     seq = lax.axis_index("seq")
     tp = lax.axis_index("tp")
@@ -65,30 +65,37 @@
     y_peers = [(lax.rem(y + d, RING) * 16 + z * 2 + c, tp) for d in (4, 3, 5, 2, 6, 1, 7)]
     z_peers = [(y * 16 + lax.rem(z + d, RING) * 2 + c, tp) for d in (4, 3, 5, 2, 6, 1, 7)]
     sibling = (y * 16 + z * 2 + (1 - c), tp)
+    y_zero = [(lax.rem(y + d, RING) * 16 + z * 2, tp) for d in (4, 3, 5, 2, 6, 1, 7)]
+    z_zero = [(y * 16 + lax.rem(z + d, RING) * 2, tp) for d in (4, 3, 5, 2, 6, 1, 7)]
 
     barrier = pltpu.get_barrier_semaphore()
+
     def signal(peer):
         pl.semaphore_signal(barrier, inc=1, device_id=peer, device_id_type=MESH)
 
-    for peer in tp_peers:
-        signal(peer)
-    loads[0].start()
-    for peer in [sibling] + z_peers + y_peers:
-        signal(peer)
-
     @pl.when(c == 1)
     def _():
-        loads[1].start()
-
-    for index in (8, 2, 3, 5, 6, 7):
-        loads[index].start()
-
-    @pl.when(c == 1)
-    def _():
-        loads[4].start()
-
-    loads[0].wait()
-    pl.semaphore_wait(barrier, 18)
+        for peer in tp_peers:
+            signal(peer)
+        loads[0].start()
+        for z_peer, y_peer in zip(z_zero, y_zero):
+            signal(z_peer)
+            signal(y_peer)
+        signal(sibling)
+        for index in (1, 8, 2, 3, 4, 5, 6, 7):
+            loads[index].start()
+        loads[0].wait()
+        pl.semaphore_wait(barrier, 3)
+
+    @pl.when(c == 0)
+    def _():
+        for z_peer, y_peer in zip(z_peers, y_peers):
+            signal(z_peer)
+            signal(y_peer)
+        for peer in tp_peers:
+            signal(peer)
+        for index in (8, 2, 3, 0, 5, 6, 7):
+            loads[index].start()
 
     def push(src, dst, stage, recv_sem, peer):
         pltpu.make_async_remote_copy(
@@ -129,10 +136,14 @@
             arrived(gath.at[t], hsem.at[i])
             acc = acc + project(0, t)
         qkv[0] = acc.astype(BF16)
+        pl.semaphore_wait(ready, 1)
         push(qkv.at[0], qkv.at[0], 6, recv.at[5], sibling)
 
     @pl.when(c == 0)
     def _():
+        pl.semaphore_wait(barrier, 32)
+        pl.semaphore_signal(ready, inc=1, device_id=sibling, device_id_type=MESH)
+        loads[0].wait()
         arrived(qkv.at[0], recv.at[5])
 
     query = qkv[0]
@@ -360,7 +371,7 @@
             pltpu.VMEM((2 * RING * SLOT, 128), F32),
             pltpu.VMEM((TP, HALF, D), F32),
             pltpu.VMEM((2, HALF, W), F32),
-            dma((9,)), dma((3,)), dma((7,)), dma((8,)),
+            dma((9,)), dma((3,)), dma((7,)), dma((8,)), pltpu.SemaphoreType.REGULAR,
         ],
         compiler_params=pltpu.CompilerParams(collective_id=0, has_side_effects=True),
         name="sublayer",

time: 35.7 us -> 34.7 us (0.972)
  Pallas kernels: 34.9 us -> 34 us
    pallas_call x1, Pallas kernels: 33.9 us -> 33 us  [body(): pl.pallas_call(kernel, out_shape=(pltpu.VMEM((B, W), BF16), pltpu.VMEM(ca...]
where the time goes in v7:
time: 34.7 us; the launch traced here: 34.6 us
  Pallas kernels  34 us (98%)
  between operations  0.64 us (2%)
    pallas_call x1, Pallas kernels, body(): pl.pallas_call(kernel, out_shape=(pltpu.VMEM((B, W), BF16), pltpu.VMEM(ca...  33 us
    pallas_call x1, Pallas kernels, body(): pl.pallas_call(hand_out, out_shape=(jax.ShapeDtypeStruct((B, W), BF16), j...  1 us

profile of v7, /device:TPU:1, one launch (start us, length us, event | category | flops | bytes accessed | tf_op | source)
XLA Modules:
  0.0 34.6 jit_solution(17155361518180382429)
XLA Ops:
  0.6 33.0 %sublayer.1 = (bf16[16,256]{1,0:T(8,128)(2,1)S(1)}, bf16[16,64,256]{2,1,0:T(8,128)(2,1)S(1)}, bf16[16,64,256]{2,1,0:T(8,128)(2,1)S(1)}) custom-call(s32[16]{0:T(128)} %lengths.1, bf16[16,256]{1,0:T(8,128)(2,1)} %hid.1, bf16[3,1024,256]{2,1,0:T(8,128)(2,1)} %wqkv.1, bf16[256,1024]{1,0:T(8,128)(2,1)} %wout.1, bf16[16,64,256]{2,1,0:T(8,128)(2,1)} %kc.1, ...), custom_call_target="tpu_custom_call" | custom-call | tf_op jit(solution)/shard_map/sublayer/pallas_call | solution.py:355
  33.6 1.0 %hand_out.1 = (bf16[16,256]{1,0:T(8,128)(2,1)}, bf16[16,64,256]{2,1,0:T(8,128)(2,1)}, bf16[16,64,256]{2,1,0:T(8,128)(2,1)}) custom-call(bf16[16,256]{1,0:T(8,128)(2,1)S(1)} %get-tuple-element.6.o_in, bf16[16,64,256]{2,1,0:T(8,128)(2,1)S(1)} %get-tuple-element.7.k_in, bf16[16,64,256]{2,1,0:T(8,128)(2,1)S(1)} %get-tuple-element.8.v_in), custom_call_target="tpu_custom_call" | custom-call | tf_op jit(solution)/shard_map/hand_out/pallas_call | solution.py:382

commit v8 on v7

--- a/solution.py
+++ b/solution.py
@@ -42,7 +42,7 @@
 def kernel(
     lengths, hid, wqkv, wout, kc, vc, gain, bias,
     out, kbuf, vbuf,
-    lens, gath, qkv, wbuf, wobuf, gbuf, bbuf,
+    lens, across, gath, qkv, wbuf, wobuf, gbuf, bbuf,
     csend, crecv, yb, zb, mixb, fin,
     lsem, hsem, recv, sent, ready,
 ):
@@ -125,6 +125,8 @@
     lane = iota((4 * B, 128), 1)
     valid = jnp.logical_and(lane // SPAN == request % 2, lane % SPAN < row_len)
     pair = request // 2
+    loads[2].wait()
+    across[...] = kbuf[...].reshape(B * SPAN, W).T
     same_head = jnp.where(iota((128, 128), 0) // HD == iota((128, 128), 1) // HD, 1.0, 0.0).astype(BF16)
 
     @pl.when(c == 1)
@@ -151,9 +153,7 @@
     spread = jnp.concatenate(
         [jnp.where(column_head == h, query.astype(F32), 0.0) for h in range(4)], axis=0
     ).astype(BF16)
-    loads[2].wait()
-    keys = kbuf[...].reshape(B * SPAN, W)
-    every = lax.dot_general(spread, keys, (((1,), (1,)), ((), ())), preferred_element_type=F32)
+    every = jnp.dot(spread, across[...], preferred_element_type=F32)
     scores = every[:, :128]
     for j in range(1, 8):
         scores = jnp.where(pair == j, every[:, j * 128 : j * 128 + 128], scores)
@@ -339,8 +339,11 @@
 
 
 def hand_out(o_in, k_in, v_in, o_out, k_out, v_out, sem):
-    pairs = ((k_in, k_out), (v_in, v_out), (o_in, o_out))
-    copies = [pltpu.make_async_copy(a, b, sem.at[i]) for i, (a, b) in enumerate(pairs)]
+    copies = [pltpu.make_async_copy(o_in, o_out, sem.at[0])]
+    for i in range(4):
+        part = pl.ds(i * B // 4, B // 4)
+        copies.append(pltpu.make_async_copy(k_in.at[part], k_out.at[part], sem.at[1 + 2 * i]))
+        copies.append(pltpu.make_async_copy(v_in.at[part], v_out.at[part], sem.at[2 + 2 * i]))
     for copy in copies:
         copy.start()
     for copy in copies:
@@ -359,6 +362,7 @@
         out_specs=(vmem, vmem, vmem),
         scratch_shapes=[
             pltpu.SMEM((B,), jnp.int32),
+            pltpu.VMEM((W, B * SPAN), BF16),
             pltpu.VMEM((TP, B, W), BF16),
             pltpu.VMEM((3, B, W), BF16),
             pltpu.VMEM((3, D, W), BF16),
@@ -388,7 +392,7 @@
         ),
         in_specs=[vmem] * 3,
         out_specs=(hbm, hbm, hbm),
-        scratch_shapes=[dma((3,))],
+        scratch_shapes=[dma((9,))],
         name="hand_out",
     )(*[pltpu.with_memory_space_constraint(part, pltpu.VMEM) for part in done])
 

time: 34.7 us -> 34.7 us (level)
  no operation moved by 1% of the time
where the time goes in v8:
time: 34.7 us; the launch traced here: 34.6 us
  Pallas kernels  33.9 us (98%)
  between operations  0.64 us (2%)
    pallas_call x1, Pallas kernels, body(): pl.pallas_call(kernel, out_shape=(pltpu.VMEM((B, W), BF16), pltpu.VMEM(ca...  32.9 us
    pallas_call x1, Pallas kernels, body(): pl.pallas_call(hand_out, out_shape=(jax.ShapeDtypeStruct((B, W), BF16), j...  1.04 us

profile of v8, /device:TPU:1, one launch (start us, length us, event | category | flops | bytes accessed | tf_op | source)
XLA Modules:
  0.0 34.6 jit_solution(3202115013717563859)
XLA Ops:
  0.6 32.9 %sublayer.1 = (bf16[16,256]{1,0:T(8,128)(2,1)S(1)}, bf16[16,64,256]{2,1,0:T(8,128)(2,1)S(1)}, bf16[16,64,256]{2,1,0:T(8,128)(2,1)S(1)}) custom-call(s32[16]{0:T(128)} %lengths.1, bf16[16,256]{1,0:T(8,128)(2,1)} %hid.1, bf16[3,1024,256]{2,1,0:T(8,128)(2,1)} %wqkv.1, bf16[256,1024]{1,0:T(8,128)(2,1)} %wout.1, bf16[16,64,256]{2,1,0:T(8,128)(2,1)} %kc.1, ...), custom_call_target="tpu_custom_call" | custom-call | tf_op jit(solution)/shard_map/sublayer/pallas_call | solution.py:358
  33.5 1.0 %hand_out.1 = (bf16[16,256]{1,0:T(8,128)(2,1)}, bf16[16,64,256]{2,1,0:T(8,128)(2,1)}, bf16[16,64,256]{2,1,0:T(8,128)(2,1)}) custom-call(bf16[16,256]{1,0:T(8,128)(2,1)S(1)} %get-tuple-element.6.o_in, bf16[16,64,256]{2,1,0:T(8,128)(2,1)S(1)} %get-tuple-element.7.k_in, bf16[16,64,256]{2,1,0:T(8,128)(2,1)S(1)} %get-tuple-element.8.v_in), custom_call_target="tpu_custom_call" | custom-call | tf_op jit(solution)/shard_map/hand_out/pallas_call | solution.py:386

commit v9 on v8

--- a/solution.py
+++ b/solution.py
@@ -68,31 +68,59 @@
     y_zero = [(lax.rem(y + d, RING) * 16 + z * 2, tp) for d in (4, 3, 5, 2, 6, 1, 7)]
     z_zero = [(y * 16 + lax.rem(z + d, RING) * 2, tp) for d in (4, 3, 5, 2, 6, 1, 7)]
 
+    t_zero = [(y * 16 + z * 2, peer[1]) for peer in tp_peers]
+
+    def at_z(other):
+        return (y * 16 + other * 2 + c, tp)
+
+    is_src = jnp.logical_or(z == 0, z == 3)
+    step = jnp.where(z == 3, 1, RING - 1)
+    served = [
+        at_z(lax.rem(z + RING - step, RING)),
+        at_z(lax.rem(z + step, RING)),
+        at_z(lax.rem(z + 2 * step, RING)),
+    ]
+    my_src = jnp.where(jnp.logical_or(z == 1, z >= 6), 0, 3)
+    my_index = jnp.where(z <= 2, 0, jnp.where(jnp.logical_or(z == 4, z == 7), 1, 2))
+    core0 = c == 0
+    source = jnp.logical_and(c == 1, is_src)
+    fed = jnp.logical_and(c == 1, jnp.logical_not(is_src))
+    core0_source = jnp.logical_and(core0, is_src)
+    core0_fed = jnp.logical_and(core0, jnp.logical_not(is_src))
+
     barrier = pltpu.get_barrier_semaphore()
 
-    def signal(peer):
-        pl.semaphore_signal(barrier, inc=1, device_id=peer, device_id_type=MESH)
-
-    @pl.when(c == 1)
-    def _():
-        for peer in tp_peers:
+    def signal(peer, sem=barrier):
+        pl.semaphore_signal(sem, inc=1, device_id=peer, device_id_type=MESH)
+
+    @pl.when(source)
+    def _():
+        for peer in tp_peers + served:
             signal(peer)
         loads[0].start()
-        for z_peer, y_peer in zip(z_zero, y_zero):
-            signal(z_peer)
-            signal(y_peer)
-        signal(sibling)
+        for peer in z_zero + y_zero + t_zero + [sibling]:
+            signal(peer)
         for index in (1, 8, 2, 3, 4, 5, 6, 7):
             loads[index].start()
         loads[0].wait()
-        pl.semaphore_wait(barrier, 3)
-
-    @pl.when(c == 0)
-    def _():
-        for z_peer, y_peer in zip(z_peers, y_peers):
-            signal(z_peer)
-            signal(y_peer)
-        for peer in tp_peers:
+        pl.semaphore_wait(barrier, 4)
+
+    @pl.when(fed)
+    def _():
+        pl.semaphore_wait(barrier, 1)
+        signal(at_z(my_src), ready.at[my_index])
+        for peer in z_zero + y_zero + t_zero + [sibling]:
+            signal(peer)
+        for index in (8, 2, 3, 0, 5, 6, 7):
+            loads[index].start()
+
+    @pl.when(core0_source)
+    def _():
+        signal(sibling)
+
+    @pl.when(core0)
+    def _():
+        for peer in z_peers + y_peers + tp_peers:
             signal(peer)
         for index in (8, 2, 3, 0, 5, 6, 7):
             loads[index].start()
@@ -109,7 +137,11 @@
         rows = pl.ds(pl.multiple_of(t * W, W), W)
         return jnp.dot(gath[t], wbuf[index, rows, :], preferred_element_type=F32)
 
-    @pl.when(c == 1)
+    def tell_core1():
+        pl.semaphore_wait(barrier, 35)
+        signal(sibling, ready.at[3])
+
+    @pl.when(source)
     def _():
         for i, peer in enumerate(tp_peers):
             push(gath.at[tp], gath.at[tp], 0, hsem.at[i], peer)
@@ -129,7 +161,7 @@
     across[...] = kbuf[...].reshape(B * SPAN, W).T
     same_head = jnp.where(iota((128, 128), 0) // HD == iota((128, 128), 1) // HD, 1.0, 0.0).astype(BF16)
 
-    @pl.when(c == 1)
+    @pl.when(source)
     def _():
         loads[1].wait()
         acc = project(0, tp)
@@ -138,14 +170,28 @@
             arrived(gath.at[t], hsem.at[i])
             acc = acc + project(0, t)
         qkv[0] = acc.astype(BF16)
-        pl.semaphore_wait(ready, 1)
         push(qkv.at[0], qkv.at[0], 6, recv.at[5], sibling)
-
-    @pl.when(c == 0)
-    def _():
-        pl.semaphore_wait(barrier, 32)
-        pl.semaphore_signal(ready, inc=1, device_id=sibling, device_id_type=MESH)
-        loads[0].wait()
+        loads[4].wait()
+        for index in (1, 2):
+            qkv[index] = sum(project(index, t) for t in range(TP)).astype(BF16)
+        push(qkv.at[pl.ds(1, 2)], qkv.at[pl.ds(1, 2)], 7, recv.at[6], sibling)
+        for i in range(3):
+            pl.semaphore_wait(ready.at[i], 1)
+            push(qkv.at[0], qkv.at[0], 6, recv.at[5], served[i])
+            push(qkv.at[pl.ds(1, 2)], qkv.at[pl.ds(1, 2)], 7, recv.at[6], served[i])
+
+    @pl.when(fed)
+    def _():
+        arrived(qkv.at[0], recv.at[5])
+        pl.semaphore_wait(ready.at[3], 1)
+        push(qkv.at[0], qkv.at[0], 6, recv.at[5], sibling)
+
+    @pl.when(core0_fed)
+    def _():
+        tell_core1()
+
+    @pl.when(core0)
+    def _():
         arrived(qkv.at[0], recv.at[5])
 
     query = qkv[0]
@@ -185,11 +231,9 @@
             csend[core, i] = part[core * HALF : (core + 1) * HALF]
     push(csend.at[1 - c], crecv, 1, recv.at[0], sibling)
 
-    @pl.when(c == 1)
-    def _():
-        loads[4].wait()
-        for index in (1, 2):
-            qkv[index] = sum(project(index, t) for t in range(TP)).astype(BF16)
+    @pl.when(fed)
+    def _():
+        arrived(qkv.at[pl.ds(1, 2)], recv.at[6])
         push(qkv.at[pl.ds(1, 2)], qkv.at[pl.ds(1, 2)], 7, recv.at[6], sibling)
 
     arrived(crecv, recv.at[0])
@@ -237,11 +281,24 @@
     low_row, high_row = to_row(both_top, both_total)
     place(yb, y, both_acc[:, :128], low_row)
     place(yb, RING + z, both_acc[:, 128:], high_row)
+
+    @pl.when(core0_source)
+    def _():
+        tell_core1()
+
+    @pl.when(source)
+    def _():
+        pl.semaphore_wait(ready.at[3], 1)
+
     push_ring(yb, y, RING + z, 2, recv.at[1])
 
-    @pl.when(c == 0)
+    @pl.when(core0)
     def _():
         arrived(qkv.at[pl.ds(1, 2)], recv.at[6])
+
+    @pl.when(jnp.logical_not(source))
+    def _():
+        loads[0].wait()
 
     new_key, new_value = qkv[1], qkv[2]
     product = query.astype(F32) * new_key.astype(F32)
@@ -323,9 +380,14 @@
     fin[c] = own / jnp.sqrt(var + 1e-05) * gbuf[...] + bbuf[...]
     push(fin.at[c], fin.at[c], 5, recv.at[4], sibling)
 
-    @pl.when(c == 1)
+    @pl.when(source)
     def _():
         arrived(gath.at[pl.ds(0, 3)], sent.at[0])
+        arrived(gath, sent.at[6])
+        arrived(wbuf.at[0, pl.ds(0, 8 * B), :], sent.at[7])
+
+    @pl.when(fed)
+    def _():
         arrived(qkv.at[0], sent.at[6])
         arrived(qkv.at[pl.ds(1, 2)], sent.at[7])
 
@@ -375,7 +437,7 @@
             pltpu.VMEM((2 * RING * SLOT, 128), F32),
             pltpu.VMEM((TP, HALF, D), F32),
             pltpu.VMEM((2, HALF, W), F32),
-            dma((9,)), dma((3,)), dma((7,)), dma((8,)), pltpu.SemaphoreType.REGULAR,
+            dma((9,)), dma((3,)), dma((7,)), dma((8,)), pltpu.SemaphoreType.REGULAR((4,)),
         ],
         compiler_params=pltpu.CompilerParams(collective_id=0, has_side_effects=True),
         name="sublayer",

time: 34.7 us -> 35.4 us (1.020)
  Pallas kernels: 33.9 us -> 34.6 us
    pallas_call x1, Pallas kernels: 32.9 us -> 33.6 us  [body(): pl.pallas_call(kernel, out_shape=(pltpu.VMEM((B, W), BF16), pltpu.VMEM(ca...]
where the time goes in v9:
time: 35.4 us; the launch traced here: 35.3 us
  Pallas kernels  34.6 us (98%)
  between operations  0.64 us (2%)
    pallas_call x1, Pallas kernels, body(): pl.pallas_call(kernel, out_shape=(pltpu.VMEM((B, W), BF16), pltpu.VMEM(ca...  33.6 us
    pallas_call x1, Pallas kernels, body(): pl.pallas_call(hand_out, out_shape=(jax.ShapeDtypeStruct((B, W), BF16), j...  1.04 us

profile of v9, /device:TPU:1, one launch (start us, length us, event | category | flops | bytes accessed | tf_op | source)
XLA Modules:
  0.0 35.3 jit_solution(14798674389962380950)
XLA Ops:
  0.6 33.6 %sublayer.1 = (bf16[16,256]{1,0:T(8,128)(2,1)S(1)}, bf16[16,64,256]{2,1,0:T(8,128)(2,1)S(1)}, bf16[16,64,256]{2,1,0:T(8,128)(2,1)S(1)}) custom-call(s32[16]{0:T(128)} %lengths.1, bf16[16,256]{1,0:T(8,128)(2,1)} %hid.1, bf16[3,1024,256]{2,1,0:T(8,128)(2,1)} %wqkv.1, bf16[256,1024]{1,0:T(8,128)(2,1)} %wout.1, bf16[16,64,256]{2,1,0:T(8,128)(2,1)} %kc.1, ...), custom_call_target="tpu_custom_call" | custom-call | tf_op jit(solution)/shard_map/sublayer/pallas_call | solution.py:420
  34.2 1.0 %hand_out.1 = (bf16[16,256]{1,0:T(8,128)(2,1)}, bf16[16,64,256]{2,1,0:T(8,128)(2,1)}, bf16[16,64,256]{2,1,0:T(8,128)(2,1)}) custom-call(bf16[16,256]{1,0:T(8,128)(2,1)S(1)} %get-tuple-element.6.o_in, bf16[16,64,256]{2,1,0:T(8,128)(2,1)S(1)} %get-tuple-element.7.k_in, bf16[16,64,256]{2,1,0:T(8,128)(2,1)S(1)} %get-tuple-element.8.v_in), custom_call_target="tpu_custom_call" | custom-call | tf_op jit(solution)/shard_map/hand_out/pallas_call | solution.py:448

commit v10 on v8

--- a/solution.py
+++ b/solution.py
@@ -85,10 +85,11 @@
         for index in (1, 8, 2, 3, 4, 5, 6, 7):
             loads[index].start()
         loads[0].wait()
-        pl.semaphore_wait(barrier, 3)
+        pl.semaphore_wait(barrier, 4)
 
     @pl.when(c == 0)
     def _():
+        signal(sibling)
         for z_peer, y_peer in zip(z_peers, y_peers):
             signal(z_peer)
             signal(y_peer)
@@ -138,13 +139,10 @@
             arrived(gath.at[t], hsem.at[i])
             acc = acc + project(0, t)
         qkv[0] = acc.astype(BF16)
-        pl.semaphore_wait(ready, 1)
         push(qkv.at[0], qkv.at[0], 6, recv.at[5], sibling)
 
     @pl.when(c == 0)
     def _():
-        pl.semaphore_wait(barrier, 32)
-        pl.semaphore_signal(ready, inc=1, device_id=sibling, device_id_type=MESH)
         loads[0].wait()
         arrived(qkv.at[0], recv.at[5])
 
@@ -192,6 +190,11 @@
             qkv[index] = sum(project(index, t) for t in range(TP)).astype(BF16)
         push(qkv.at[pl.ds(1, 2)], qkv.at[pl.ds(1, 2)], 7, recv.at[6], sibling)
 
+    @pl.when(c == 0)
+    def _():
+        pl.semaphore_wait(barrier, 32)
+        pl.semaphore_signal(ready, inc=1, device_id=sibling, device_id_type=MESH)
+
     arrived(crecv, recv.at[0])
     my_acc, my_total, my_top = csend[c, 0], csend[c, 1], csend[c, 2]
     both_top = jnp.maximum(my_top, crecv[2])
@@ -237,6 +240,11 @@
     low_row, high_row = to_row(both_top, both_total)
     place(yb, y, both_acc[:, :128], low_row)
     place(yb, RING + z, both_acc[:, 128:], high_row)
+
+    @pl.when(c == 1)
+    def _():
+        pl.semaphore_wait(ready, 1)
+
     push_ring(yb, y, RING + z, 2, recv.at[1])
 
     @pl.when(c == 0)

time: 34.7 us -> 34.8 us (level)
  no operation moved by 1% of the time
where the time goes in v10:
time: 34.8 us; the launch traced here: 34.6 us
  Pallas kernels  34 us (98%)
  between operations  0.64 us (2%)
    pallas_call x1, Pallas kernels, body(): pl.pallas_call(kernel, out_shape=(pltpu.VMEM((B, W), BF16), pltpu.VMEM(ca...  32.9 us
    pallas_call x1, Pallas kernels, body(): pl.pallas_call(hand_out, out_shape=(jax.ShapeDtypeStruct((B, W), BF16), j...  1.04 us

profile of v10, /device:TPU:1, one launch (start us, length us, event | category | flops | bytes accessed | tf_op | source)
XLA Modules:
  0.0 34.6 jit_solution(5589177406864178076)
XLA Ops:
  0.6 32.9 %sublayer.1 = (bf16[16,256]{1,0:T(8,128)(2,1)S(1)}, bf16[16,64,256]{2,1,0:T(8,128)(2,1)S(1)}, bf16[16,64,256]{2,1,0:T(8,128)(2,1)S(1)}) custom-call(s32[16]{0:T(128)} %lengths.1, bf16[16,256]{1,0:T(8,128)(2,1)} %hid.1, bf16[3,1024,256]{2,1,0:T(8,128)(2,1)} %wqkv.1, bf16[256,1024]{1,0:T(8,128)(2,1)} %wout.1, bf16[16,64,256]{2,1,0:T(8,128)(2,1)} %kc.1, ...), custom_call_target="tpu_custom_call" | custom-call | tf_op jit(solution)/shard_map/sublayer/pallas_call | solution.py:366
  33.6 1.0 %hand_out.1 = (bf16[16,256]{1,0:T(8,128)(2,1)}, bf16[16,64,256]{2,1,0:T(8,128)(2,1)}, bf16[16,64,256]{2,1,0:T(8,128)(2,1)}) custom-call(bf16[16,256]{1,0:T(8,128)(2,1)S(1)} %get-tuple-element.6.o_in, bf16[16,64,256]{2,1,0:T(8,128)(2,1)S(1)} %get-tuple-element.7.k_in, bf16[16,64,256]{2,1,0:T(8,128)(2,1)S(1)} %get-tuple-element.8.v_in), custom_call_target="tpu_custom_call" | custom-call | tf_op jit(solution)/shard_map/hand_out/pallas_call | solution.py:394

commit v11 on v10

--- a/solution.py
+++ b/solution.py
@@ -43,7 +43,7 @@
     lengths, hid, wqkv, wout, kc, vc, gain, bias,
     out, kbuf, vbuf,
     lens, across, gath, qkv, wbuf, wobuf, gbuf, bbuf,
-    csend, crecv, yb, zb, mixb, fin,
+    csend, crecv, staged, yb, zb, mixb, fin,
     lsem, hsem, recv, sent, ready,
 ):
     seq = lax.axis_index("seq")
@@ -67,6 +67,9 @@
     sibling = (y * 16 + z * 2 + (1 - c), tp)
     y_zero = [(lax.rem(y + d, RING) * 16 + z * 2, tp) for d in (4, 3, 5, 2, 6, 1, 7)]
     z_zero = [(y * 16 + lax.rem(z + d, RING) * 2, tp) for d in (4, 3, 5, 2, 6, 1, 7)]
+
+    y_one = [(peer[0] + 1, tp) for peer in y_zero]
+    z_one = [(peer[0] + 1, tp) for peer in z_zero]
 
     barrier = pltpu.get_barrier_semaphore()
 
@@ -181,7 +184,10 @@
     for core in range(2):
         for i, part in enumerate((fold(summed), fold(total), fold(top))):
             csend[core, i] = part[core * HALF : (core + 1) * HALF]
-    push(csend.at[1 - c], crecv, 1, recv.at[0], sibling)
+
+    @pl.when(c == 1)
+    def _():
+        push(csend, crecv, 1, recv.at[0], sibling)
 
     @pl.when(c == 1)
     def _():
@@ -195,13 +201,6 @@
         pl.semaphore_wait(barrier, 32)
         pl.semaphore_signal(ready, inc=1, device_id=sibling, device_id_type=MESH)
 
-    arrived(crecv, recv.at[0])
-    my_acc, my_total, my_top = csend[c, 0], csend[c, 1], csend[c, 2]
-    both_top = jnp.maximum(my_top, crecv[2])
-    mine, other = jnp.exp(my_top - both_top), jnp.exp(crecv[2] - both_top)
-    both_acc = my_acc * mine + crecv[0] * other
-    both_total = my_total * mine + crecv[1] * other
-
     def place(ref, slot, acc, row):
         base = pl.multiple_of(slot * SLOT, 8)
         ref[pl.ds(base, 8), :] = acc
@@ -210,8 +209,8 @@
     def slot_of(ref, slot):
         return ref.at[pl.ds(pl.multiple_of(slot * SLOT, 8), SENT), :]
 
-    def wait_ring(ref, sem):
-        arrived(ref.at[pl.ds(0, 14 * SENT), :], sem)
+    def wait_ring(ref, sem, slots=14):
+        arrived(ref.at[pl.ds(0, slots * SENT), :], sem)
 
     def push_ring(ref, slot_y, slot_z, stage, recv_sem):
         for y_peer, z_peer in zip(y_peers, z_peers):
@@ -237,15 +236,24 @@
     def over(first, second):
         return jnp.where(iota((2 * RING, 128), 0) < RING, first, second)
 
-    low_row, high_row = to_row(both_top, both_total)
-    place(yb, y, both_acc[:, :128], low_row)
-    place(yb, RING + z, both_acc[:, 128:], high_row)
-
-    @pl.when(c == 1)
-    def _():
-        pl.semaphore_wait(ready, 1)
-
-    push_ring(yb, y, RING + z, 2, recv.at[1])
+    @pl.when(c == 0)
+    def _():
+        arrived(crecv, recv.at[0])
+        for core, ref, low_slot, high_slot in ((0, yb, y, RING + z), (1, staged, 0, 1)):
+            both_top = jnp.maximum(csend[core, 2], crecv[core, 2])
+            mine, other = jnp.exp(csend[core, 2] - both_top), jnp.exp(crecv[core, 2] - both_top)
+            both_acc = csend[core, 0] * mine + crecv[core, 0] * other
+            both_total = csend[core, 1] * mine + crecv[core, 1] * other
+            low_row, high_row = to_row(both_top, both_total)
+            place(ref, low_slot, both_acc[:, :128], low_row)
+            place(ref, high_slot, both_acc[:, 128:], high_row)
+        for i in range(RING - 1):
+            push(slot_of(yb, y), slot_of(yb, y), 2, recv.at[1], y_peers[i])
+            push(slot_of(yb, RING + z), slot_of(yb, RING + z), 2, recv.at[1], z_peers[i])
+            push(slot_of(staged, 0), slot_of(yb, y), 2, recv.at[1], y_one[i])
+            push(slot_of(staged, 1), slot_of(yb, RING + z), 2, recv.at[1], z_one[i])
+        push(slot_of(staged, 0), slot_of(yb, y), 2, recv.at[1], sibling)
+        push(slot_of(staged, 1), slot_of(yb, RING + z), 2, recv.at[1], sibling)
 
     @pl.when(c == 0)
     def _():
@@ -267,7 +275,15 @@
         kbuf[b] = jnp.where(hit, new_key[b : b + 1].astype(F32), kbuf[b].astype(F32)).astype(BF16)
         vbuf[b] = jnp.where(hit, new_value[b : b + 1].astype(F32), vbuf[b].astype(F32)).astype(BF16)
     max_lane = iota((1, 128), 1) % HD < HALF
-    wait_ring(yb, recv.at[1])
+
+    @pl.when(c == 0)
+    def _():
+        wait_ring(yb, recv.at[1])
+
+    @pl.when(c == 1)
+    def _():
+        wait_ring(yb, recv.at[1], 16)
+
     rows = yb[pl.ds(8, 2 * RING, stride=SLOT), :]
     low_top = jnp.max(rows[:RING], axis=0, keepdims=True)
     high_top = jnp.max(rows[RING:], axis=0, keepdims=True)
@@ -278,6 +294,11 @@
     factors = spread_rows(factor)
     place(zb, z, ring_acc(yb, factors, 0), jnp.where(max_lane, low_top, low_total))
     place(zb, RING + y, ring_acc(yb, factors, RING), jnp.where(max_lane, high_top, high_total))
+
+    @pl.when(c == 1)
+    def _():
+        pl.semaphore_wait(ready, 1)
+
     push_ring(zb, RING + y, z, 3, recv.at[2])
 
     own_hidden = own_half(gath[tp].astype(F32))
@@ -337,8 +358,14 @@
         arrived(qkv.at[0], sent.at[6])
         arrived(qkv.at[pl.ds(1, 2)], sent.at[7])
 
-    arrived(crecv, sent.at[1])
-    wait_ring(yb, sent.at[2])
+    @pl.when(c == 1)
+    def _():
+        arrived(csend, sent.at[1])
+
+    @pl.when(c == 0)
+    def _():
+        arrived(yb.at[pl.ds(0, 30 * SENT), :], sent.at[2])
+
     wait_ring(zb, sent.at[3])
     arrived(mixb.at[pl.ds(0, 3)], sent.at[4])
     arrived(fin.at[0], recv.at[4])
@@ -378,8 +405,9 @@
             pltpu.VMEM((1, W), F32),
             pltpu.VMEM((1, W), F32),
             pltpu.VMEM((2, 3, HALF, W), F32),
-            pltpu.VMEM((3, HALF, W), F32),
-            pltpu.VMEM((2 * RING * SLOT, 128), F32),
+            pltpu.VMEM((2, 3, HALF, W), F32),
+            pltpu.VMEM((2 * SLOT, 128), F32),
+            pltpu.VMEM((2 * (RING + 1) * SLOT, 128), F32),
             pltpu.VMEM((2 * RING * SLOT, 128), F32),
             pltpu.VMEM((TP, HALF, D), F32),
             pltpu.VMEM((2, HALF, W), F32),

time: 34.8 us -> 35.1 us (level)
  Pallas kernels: 34 us -> 34.4 us
    pallas_call x1, Pallas kernels: 32.9 us -> 33.3 us  [body(): pl.pallas_call(kernel, out_shape=(pltpu.VMEM((B, W), BF16), pltpu.VMEM(ca...]
where the time goes in v11:
time: 35.1 us; the launch traced here: 35 us
  Pallas kernels  34.4 us (98%)
  between operations  0.64 us (2%)
    pallas_call x1, Pallas kernels, body(): pl.pallas_call(kernel, out_shape=(pltpu.VMEM((B, W), BF16), pltpu.VMEM(ca...  33.3 us
    pallas_call x1, Pallas kernels, body(): pl.pallas_call(hand_out, out_shape=(jax.ShapeDtypeStruct((B, W), BF16), j...  1.04 us

profile of v11, /device:TPU:1, one launch (start us, length us, event | category | flops | bytes accessed | tf_op | source)
XLA Modules:
  0.0 35.0 jit_solution(6497035084100790947)
XLA Ops:
  0.6 33.3 %sublayer.1 = (bf16[16,256]{1,0:T(8,128)(2,1)S(1)}, bf16[16,64,256]{2,1,0:T(8,128)(2,1)S(1)}, bf16[16,64,256]{2,1,0:T(8,128)(2,1)S(1)}) custom-call(s32[16]{0:T(128)} %lengths.1, bf16[16,256]{1,0:T(8,128)(2,1)} %hid.1, bf16[3,1024,256]{2,1,0:T(8,128)(2,1)} %wqkv.1, bf16[256,1024]{1,0:T(8,128)(2,1)} %wout.1, bf16[16,64,256]{2,1,0:T(8,128)(2,1)} %kc.1, ...), custom_call_target="tpu_custom_call" | custom-call | tf_op jit(solution)/shard_map/sublayer/pallas_call | solution.py:393
  34.0 1.0 %hand_out.1 = (bf16[16,256]{1,0:T(8,128)(2,1)}, bf16[16,64,256]{2,1,0:T(8,128)(2,1)}, bf16[16,64,256]{2,1,0:T(8,128)(2,1)}) custom-call(bf16[16,256]{1,0:T(8,128)(2,1)S(1)} %get-tuple-element.6.o_in, bf16[16,64,256]{2,1,0:T(8,128)(2,1)S(1)} %get-tuple-element.7.k_in, bf16[16,64,256]{2,1,0:T(8,128)(2,1)S(1)} %get-tuple-element.8.v_in), custom_call_target="tpu_custom_call" | custom-call | tf_op jit(solution)/shard_map/hand_out/pallas_call | solution.py:422

commit v12 on v10

--- a/solution.py
+++ b/solution.py
@@ -308,14 +308,21 @@
         axis=1,
     )
     attended = attended.astype(BF16)
+
+    def push_rows(half, peer):
+        part = mixb.at[tp, :, pl.ds(half * 2 * W, 2 * W)]
+        push(part, part, 4, recv.at[3], peer)
+
     for half in range(2):
         lanes = slice(half * 2 * W, (half + 1) * 2 * W)
         mixed = jnp.dot(attended, wobuf[:, lanes], preferred_element_type=F32)
         for t in (2 * half, 2 * half + 1):
             part = mixed[:, t % 2 * W : (t % 2 + 1) * W]
             mixb[tp, :, t * W : (t + 1) * W] = part + jnp.where(tp == t, own_hidden, 0.0)
-        for peer in tp_peers:
-            push(mixb.at[tp, :, pl.ds(half * 2 * W, 2 * W)], mixb.at[tp, :, pl.ds(half * 2 * W, 2 * W)], 4, recv.at[3], peer)
+        push_rows(half, tp_peers[0])
+    for half in range(2):
+        for peer in tp_peers[1:]:
+            push_rows(half, peer)
     arrived(mixb.at[pl.ds(0, 3)], recv.at[3])
     resid = []
     for t in range(TP):

time: 34.8 us -> 34.9 us (level)
  no operation moved by 1% of the time
where the time goes in v12:
time: 34.9 us; the launch traced here: 34.7 us
  Pallas kernels  34.1 us (98%)
  between operations  0.64 us (2%)
    pallas_call x1, Pallas kernels, body(): pl.pallas_call(kernel, out_shape=(pltpu.VMEM((B, W), BF16), pltpu.VMEM(ca...  33.1 us
    pallas_call x1, Pallas kernels, body(): pl.pallas_call(hand_out, out_shape=(jax.ShapeDtypeStruct((B, W), BF16), j...  1.04 us

profile of v12, /device:TPU:1, one launch (start us, length us, event | category | flops | bytes accessed | tf_op | source)
XLA Modules:
  0.0 34.7 jit_solution(15147917031358008327)
XLA Ops:
  0.6 33.1 %sublayer.1 = (bf16[16,256]{1,0:T(8,128)(2,1)S(1)}, bf16[16,64,256]{2,1,0:T(8,128)(2,1)S(1)}, bf16[16,64,256]{2,1,0:T(8,128)(2,1)S(1)}) custom-call(s32[16]{0:T(128)} %lengths.1, bf16[16,256]{1,0:T(8,128)(2,1)} %hid.1, bf16[3,1024,256]{2,1,0:T(8,128)(2,1)} %wqkv.1, bf16[256,1024]{1,0:T(8,128)(2,1)} %wout.1, bf16[16,64,256]{2,1,0:T(8,128)(2,1)} %kc.1, ...), custom_call_target="tpu_custom_call" | custom-call | tf_op jit(solution)/shard_map/sublayer/pallas_call | solution.py:373
  33.7 1.0 %hand_out.1 = (bf16[16,256]{1,0:T(8,128)(2,1)}, bf16[16,64,256]{2,1,0:T(8,128)(2,1)}, bf16[16,64,256]{2,1,0:T(8,128)(2,1)}) custom-call(bf16[16,256]{1,0:T(8,128)(2,1)S(1)} %get-tuple-element.6.o_in, bf16[16,64,256]{2,1,0:T(8,128)(2,1)S(1)} %get-tuple-element.7.k_in, bf16[16,64,256]{2,1,0:T(8,128)(2,1)S(1)} %get-tuple-element.8.v_in), custom_call_target="tpu_custom_call" | custom-call | tf_op jit(solution)/shard_map/hand_out/pallas_call | solution.py:401

commit v13 on v10

--- a/solution.py
+++ b/solution.py
@@ -314,8 +314,8 @@
         for t in (2 * half, 2 * half + 1):
             part = mixed[:, t % 2 * W : (t % 2 + 1) * W]
             mixb[tp, :, t * W : (t + 1) * W] = part + jnp.where(tp == t, own_hidden, 0.0)
-        for peer in tp_peers:
-            push(mixb.at[tp, :, pl.ds(half * 2 * W, 2 * W)], mixb.at[tp, :, pl.ds(half * 2 * W, 2 * W)], 4, recv.at[3], peer)
+    for peer in tp_peers:
+        push(mixb.at[tp], mixb.at[tp], 4, recv.at[3], peer)
     arrived(mixb.at[pl.ds(0, 3)], recv.at[3])
     resid = []
     for t in range(TP):

time: 34.8 us -> 34.8 us (level)
  no operation moved by 1% of the time
where the time goes in v13:
time: 34.8 us; the launch traced here: 34.6 us
  Pallas kernels  34 us (98%)
  between operations  0.64 us (2%)
    pallas_call x1, Pallas kernels, body(): pl.pallas_call(kernel, out_shape=(pltpu.VMEM((B, W), BF16), pltpu.VMEM(ca...  32.9 us
    pallas_call x1, Pallas kernels, body(): pl.pallas_call(hand_out, out_shape=(jax.ShapeDtypeStruct((B, W), BF16), j...  1.04 us

profile of v13, /device:TPU:1, one launch (start us, length us, event | category | flops | bytes accessed | tf_op | source)
XLA Modules:
  0.0 34.6 jit_solution(2093119817572489949)
XLA Ops:
  0.6 32.9 %sublayer.1 = (bf16[16,256]{1,0:T(8,128)(2,1)S(1)}, bf16[16,64,256]{2,1,0:T(8,128)(2,1)S(1)}, bf16[16,64,256]{2,1,0:T(8,128)(2,1)S(1)}) custom-call(s32[16]{0:T(128)} %lengths.1, bf16[16,256]{1,0:T(8,128)(2,1)} %hid.1, bf16[3,1024,256]{2,1,0:T(8,128)(2,1)} %wqkv.1, bf16[256,1024]{1,0:T(8,128)(2,1)} %wout.1, bf16[16,64,256]{2,1,0:T(8,128)(2,1)} %kc.1, ...), custom_call_target="tpu_custom_call" | custom-call | tf_op jit(solution)/shard_map/sublayer/pallas_call | solution.py:366
  33.6 1.0 %hand_out.1 = (bf16[16,256]{1,0:T(8,128)(2,1)}, bf16[16,64,256]{2,1,0:T(8,128)(2,1)}, bf16[16,64,256]{2,1,0:T(8,128)(2,1)}) custom-call(bf16[16,256]{1,0:T(8,128)(2,1)S(1)} %get-tuple-element.6.o_in, bf16[16,64,256]{2,1,0:T(8,128)(2,1)S(1)} %get-tuple-element.7.k_in, bf16[16,64,256]{2,1,0:T(8,128)(2,1)S(1)} %get-tuple-element.8.v_in), custom_call_target="tpu_custom_call" | custom-call | tf_op jit(solution)/shard_map/hand_out/pallas_call | solution.py:394
